TPU v7x, 256 devices: a whole 4x4x8 slice. The times are simulated.
256 devices in a mesh: wide: 32 (over x, y, core), narrow: 8 (over z).
Axes of the slice: x: 4, y: 4, z: 8, core: 2. Of those that a mesh axis runs over, the one named last changes fastest.
Arguments:
- blocks: bfloat16 [32, 8, 16, 64, 4096], P('wide', 'narrow'), may hold values from -16 to 16
- row_tile: int32 [32, 8, 16], P('wide', 'narrow'), may hold values from 0 to 15
- col_tile: int32 [32, 8, 16], P('wide', 'narrow'), may hold values from 0 to 63, as said below
- depth_tile: int32 [32, 8, 16], P('wide', 'narrow'), may hold values from 0 to 15
- block_count: int32 [32, 8], P('wide', 'narrow'), may hold values from 4 to 16, as said below
- factor_b: bfloat16 [32768, 256], P(('wide', 'narrow')), may hold values from -40 to 40
- factor_c: bfloat16 [1024, 256], replicated, may hold values from -0.076293945 to 0.076293945
Outputs:
- a_new: float32 [32768, 256], P(('wide', 'narrow'))
- b_new: float32 [32768, 256], P(('wide', 'narrow'))
Inputs may be any that keep to these rules, and one draw needn't show every extreme that they name: `block_count`: every device holds at least 4 live blocks, and some device exactly 16. col_tile // 2 is the index of wide that holds the block's mode-2 factor rows; among the 16 slots of one device, live or not, each such index appears at most 1 times, and some index exactly 1 times.
All inputs are finite; a program needn't handle non-finite values.
Results may differ from a plain program's by a relative error of at most 0.02.
Values may be sent and summed in bfloat16 or wider, within the bound.
No kernel may reach another device: no remote copies, remote signals or barrier semaphores. Data moves between devices by JAX's collectives and lax.ppermute only.
A program may use at most 128 MiB of HBM per device.

v0:
```python
import functools

import jax
import jax.numpy as jnp
from jax import lax
from jax.experimental import pallas as pl
from jax.experimental.pallas import tpu as pltpu
from jax.sharding import PartitionSpec as P


TI_DEV = 2
TJ_DEV = 2
NX = 4
NY = 4
NC = 2
HI = lax.Precision.HIGHEST
CHUNK = 8
PANEL = 8
UNROLL = 2
WIRE_SCALE = 32.0


def flat_wide(x, y, c):
    return ((x % NX) * NY + (y % NY)) * NC + c


def shift_wide(v, dx, dy, dc):
    pairs = []
    for x in range(NX):
        for y in range(NY):
            for c in range(NC):
                pairs.append((flat_wide(x, y, c), flat_wide(x + dx, y + dy, c ^ dc)))
    return lax.ppermute(v, "wide", pairs)


def column_gram(matrix):
    return lax.dot_general(
        matrix, matrix, (((0,), (0,)), ((), ())), preferred_element_type=jnp.float32
    )


def begin(previous, out_ref):
    @pl.when(pl.program_id(0) == 0)
    def _():
        out_ref[...] = previous[0][...] if previous else jnp.zeros_like(out_ref)


def mixed_chunk(x_ref, u, k, bs, c_rows):
    part = x_ref[u, :, k * CHUNK * bs:(k + 1) * CHUNK * bs]
    mixed = lax.dot_general(
        part, c_rows, (((0,), (0,)), ((), ())), preferred_element_type=jnp.float32
    )
    return mixed.reshape(CHUNK, bs, mixed.shape[-1])


def pass_one_kernel(first, rows_ref, picks_ref, depth_ref, count_ref, x_ref, c_ref, *rest):
    b_refs = rest[:UNROLL]
    *previous, out_ref = rest[UNROLL:]
    bs = x_ref.shape[1]
    begin(previous, out_ref)
    for u in range(UNROLL):
        slot = first + pl.program_id(0) * UNROLL + u

        @pl.when(slot < count_ref[0])
        def _():
            c_rows = c_ref[pl.ds(pl.multiple_of(depth_ref[slot] * bs, bs), bs), :]
            b_rows = b_refs[u][0].astype(jnp.float32)
            target = rows_ref[slot]
            for k in range(bs // CHUNK):
                mixed = mixed_chunk(x_ref, u, k, bs, c_rows)
                term = jnp.sum(mixed * b_rows[None, :, :], axis=1)
                out_ref[target, k * CHUNK:(k + 1) * CHUNK, :] += term


def pass_two_kernel(first, picks_ref, owners_ref, depth_ref, count_ref, x_ref, c_ref, *rest):
    a_refs = rest[:UNROLL]
    *previous, out_ref = rest[UNROLL:]
    bs = x_ref.shape[1]
    begin(previous, out_ref)
    for u in range(UNROLL):
        slot = first + pl.program_id(0) * UNROLL + u

        @pl.when(slot < count_ref[0])
        def _():
            c_rows = c_ref[pl.ds(pl.multiple_of(depth_ref[slot] * bs, bs), bs), :]
            total = jnp.zeros((bs, c_rows.shape[-1]), jnp.float32)
            for k in range(bs // CHUNK):
                mixed = mixed_chunk(x_ref, u, k, bs, c_rows)
                a_rows = a_refs[u][0, k * CHUNK:(k + 1) * CHUNK, :].astype(jnp.float32)
                total = total + jnp.sum(mixed * a_rows[:, None, :], axis=0)
            out_ref[owners_ref[slot]] = total


def run_pass(kernel, piece, pieces, tables, blocks, tiles, factor_c, out_tiles, use_first, previous=None):
    slots, bs, wide_block = blocks.shape
    rank = factor_c.shape[1]
    steps = slots // pieces // UNROLL
    start = piece * steps
    extra = [] if previous is None else [previous]

    def block_map(s, f, p, d, cnt):
        return (jnp.minimum(s + start, (cnt[0] - 1) // UNROLL), 0, 0)

    def tile_map(u, s, f, p, d, cnt):
        slot = jnp.minimum((s + start) * UNROLL + u, cnt[0] - 1)
        pick = (f if use_first else p)[slot]
        return (pick // TJ_DEV, pick % TJ_DEV, 0)

    whole = pl.BlockSpec((out_tiles, bs, rank), lambda s, f, p, d, cnt: (0, 0, 0))
    return pl.pallas_call(
        functools.partial(kernel, start * UNROLL),
        out_shape=jax.ShapeDtypeStruct((out_tiles, bs, rank), jnp.float32),
        grid_spec=pltpu.PrefetchScalarGridSpec(
            num_scalar_prefetch=4,
            grid=(steps,),
            in_specs=[
                pl.BlockSpec((UNROLL, bs, wide_block), block_map),
                pl.BlockSpec(factor_c.shape, lambda s, f, p, d, cnt: (0, 0)),
            ]
            + [
                pl.BlockSpec((1, bs, rank), functools.partial(tile_map, u)) for u in range(UNROLL)
            ]
            + [whole] * len(extra),
            out_specs=whole,
        ),
        compiler_params=pltpu.CompilerParams(dimension_semantics=("arbitrary",)),
        cost_estimate=pl.CostEstimate(
            flops=steps * UNROLL * wide_block * bs * rank * 2,
            bytes_accessed=steps * UNROLL * bs * wide_block * 2,
            transcendentals=0,
        ),
    )(*tables, blocks, factor_c, *([tiles] * UNROLL), *extra)


def mm(a, b, dims=((1,), (0,))):
    return lax.dot_general(a, b, (dims, ((), ())), precision=HI, preferred_element_type=jnp.float32)


def sweep_negated_inverse(ref):
    n = ref.shape[0]
    lane = lax.broadcasted_iota(jnp.int32, (n, n), 1)
    lane_p = lax.broadcasted_iota(jnp.int32, (PANEL, n), 1)
    sub_p = lax.broadcasted_iota(jnp.int32, (PANEL, n), 0)
    sub_1 = lax.broadcasted_iota(jnp.int32, (PANEL, 1), 0)

    def step(block, carry):
        start = pl.multiple_of(block * PANEL, PANEL)
        a = ref[...]
        panel = ref[pl.ds(start, PANEL), :]
        cols = []
        diag = []
        for j in range(PANEL):
            cols.append(jnp.sum(jnp.where(lane == start + j, a, 0.0), axis=1, keepdims=True))
            diag.append(jnp.sum(jnp.where(lane_p == start + j, panel, 0.0), axis=1, keepdims=True))
        for j in range(PANEL):
            here = lane_p == start + j
            inv = 1.0 / diag[j][j:j + 1]
            row = jnp.where(here[:1], inv, panel[j:j + 1] * inv)
            panel = jnp.where(sub_p == j, row, jnp.where(here, 0.0, panel) - diag[j] * row)
            for m in range(j + 1, PANEL):
                entry = diag[m][j:j + 1] * inv
                diag[m] = jnp.where(sub_1 == j, entry, diag[m] - diag[j] * entry)
        panel = jnp.where((lane_p >= start) & (lane_p < start + PANEL), -panel, panel)
        a = jnp.where((lane >= start) & (lane < start + PANEL), 0.0, a)
        for j in range(PANEL):
            a = a - cols[j] * panel[j:j + 1]
        ref[...] = a
        ref[pl.ds(start, PANEL), :] = panel
        return carry

    lax.fori_loop(0, n // PANEL, step, 0)
    ref[...] = -ref[...]


def unit_scale(gram, gram_c):
    rank = gram.shape[0]
    ids = jnp.arange(rank, dtype=jnp.int32)
    diag = jnp.where(ids[:, None] == ids[None, :], gram * gram_c, 0.0)
    return lax.rsqrt(jnp.sum(diag, axis=0, keepdims=True))


def invert_kernel(g_ref, c_ref, scale_ref, a1_ref, t_ref, s1_ref):
    rank = g_ref.shape[0]
    half = rank // 2
    eye = (
        lax.broadcasted_iota(jnp.int32, (rank, rank), 0)
        == lax.broadcasted_iota(jnp.int32, (rank, rank), 1)
    )
    d_row = scale_ref[...]
    d_col = jnp.sum(jnp.where(eye, d_row, 0.0), axis=1, keepdims=True)
    g = g_ref[...] * c_ref[...] * d_row * d_col
    a1_ref[...] = g[:half, :half]
    sweep_negated_inverse(a1_ref)
    b = g[half:, :half]
    t = mm(b, a1_ref[...])
    t_ref[...] = t
    s1_ref[...] = g[half:, half:] - mm(t, b, ((1,), (1,)))
    sweep_negated_inverse(s1_ref)


def invert(gram, gram_c, scale):
    half = gram.shape[0] // 2
    sq = jax.ShapeDtypeStruct((half, half), jnp.float32)
    parts = pl.pallas_call(
        invert_kernel,
        out_shape=(sq, sq, sq),
        cost_estimate=pl.CostEstimate(flops=10**10, bytes_accessed=10**6, transcendentals=0),
    )(gram, gram_c, scale)
    return (scale, *parts)


def apply_inverse(m, scale_ref, a1_ref, t_ref, s1_ref):
    half = a1_ref.shape[0]
    m1 = m[:, :half]
    z2 = mm(m[:, half:] - mm(m1, t_ref[...], ((1,), (1,))), s1_ref[...])
    z1 = mm(m1, a1_ref[...]) - mm(z2, t_ref[...])
    return jnp.concatenate([z1, z2], axis=1) * scale_ref[...]


def apply_first_kernel(m_ref, scale_ref, a1_ref, t_ref, s1_ref, out_ref, half_ref):
    m = m_ref[0]
    for k in range(1, m_ref.shape[0]):
        m = m + m_ref[k]
    z = apply_inverse(m * scale_ref[...], scale_ref, a1_ref, t_ref, s1_ref)
    out_ref[...] = z
    half_ref[...] = z.astype(jnp.bfloat16)


def apply_second_kernel(flags_ref, m_ref, scale_ref, a1_ref, t_ref, s1_ref, out_ref, acc_ref):
    acc_ref[...] = jnp.zeros_like(acc_ref)

    def step(k, carry):
        acc_ref[flags_ref[k]] += m_ref[k]
        return carry

    lax.fori_loop(0, m_ref.shape[0], step, 0)
    m = acc_ref[...].reshape(out_ref.shape) * (1.0 / WIRE_SCALE)
    out_ref[...] = apply_inverse(m, scale_ref, a1_ref, t_ref, s1_ref)


def exchange(parts, axis):
    return lax.all_to_all(parts, axis, 0, 0, tiled=True)


def roll_blocks(parts, offset):
    stacked = jnp.concatenate(parts + parts, axis=0)
    rows = parts[0].shape[0]
    return lax.dynamic_slice_in_dim(stacked, offset * rows, rows * len(parts), 0)


def gather_slices(piece, x, c):
    parts = [shift_wide(piece, k, 0, 0) for k in (3, 2, 1)] + [piece]
    mine = roll_blocks(parts, (3 - x) % NX)
    other = shift_wide(mine, 0, 0, 1)
    return jnp.concatenate(
        [jnp.where(c == 0, mine, other), jnp.where(c == 0, other, mine)], axis=0
    )


def spread(piece, count, axis):
    return exchange(jnp.broadcast_to(piece[None], (count, *piece.shape)), axis)


def local(blocks, row_tile, col_tile, depth_tile, block_count, factor_b, factor_c):
    local_blocks = blocks[0, 0]
    first_ids = row_tile[0, 0]
    second_ids = col_tile[0, 0]
    depth_ids = depth_tile[0, 0]
    count = block_count[0]
    bs = local_blocks.shape[1]
    rank = factor_c.shape[1]
    n_wide = lax.axis_size("wide")
    n_narrow = lax.axis_size("narrow")
    rows = factor_b.shape[0]
    w = lax.axis_index("wide")
    n = lax.axis_index("narrow")
    x = w // (NY * NC)
    y = (w // NC) % NY
    c = w % NC
    owners = second_ids // TJ_DEV
    inside = second_ids % TJ_DEV

    gram_c = column_gram(factor_c)

    packed = factor_b[None]
    along_x = jnp.concatenate([packed] + [shift_wide(packed, k, 0, 0) for k in (1, 2, 3)], axis=0)
    along_y = jnp.concatenate([along_x] + [shift_wide(along_x, 0, k, 0) for k in (1, 2, 3)], axis=0)
    gathered = jnp.concatenate([along_y, shift_wide(along_y, 0, 0, 1)], axis=0)

    def relative(owner):
        ox = owner // (NY * NC)
        oy = (owner // NC) % NY
        oc = owner % NC
        return ((c ^ oc) * NY + (y - oy) % NY) * NX + (x - ox) % NX

    b_pick = relative(owners) * TJ_DEV + inside
    tables = (first_ids, b_pick, depth_ids, count)

    gram_plane = column_gram(gathered.reshape(n_wide * rows, rank))
    share = rank // n_wide
    quarter = rank // (NC * NX)
    piece = lax.dynamic_slice_in_dim(gram_plane, (c * NX + x) * quarter, quarter, 0)
    arrived = spread(piece, n_narrow, "narrow")
    first_part = run_pass(
        pass_one_kernel, 0, 1, tables, local_blocks, gathered, factor_c, n_narrow * TI_DEV, False
    )
    first_part, arrived = lax.optimization_barrier((first_part, arrived))
    received = exchange(first_part.reshape(n_narrow, TI_DEV * bs, rank), "narrow")
    gram_b = gather_slices(jnp.sum(arrived, axis=0), x, c)
    factors = invert(gram_b, gram_c, unit_scale(gram_b, gram_c))
    out = jax.ShapeDtypeStruct((rows, rank), jnp.float32)
    a_new, a_half = pl.pallas_call(
        apply_first_kernel, out_shape=(out, jax.ShapeDtypeStruct((rows, rank), jnp.bfloat16))
    )(received, *factors)

    a_all = jnp.stack(
        [a_half]
        + [
            lax.ppermute(a_half, "narrow", [(i, (i + k) % n_narrow) for i in range(n_narrow)])
            for k in range(1, n_narrow)
        ]
    )
    a_pick = ((n - first_ids // TI_DEV) % n_narrow) * TI_DEV + first_ids % TI_DEV

    tables = (a_pick, owners, depth_ids, count)
    gram_w = column_gram(a_all.reshape(n_narrow * rows, rank))
    arrived = exchange(gram_w.reshape(n_wide, share, rank), "wide")
    second_part = run_pass(
        pass_two_kernel, 0, 2, tables, local_blocks, a_all, factor_c, n_wide, True
    )
    second_part, arrived = lax.optimization_barrier((second_part, arrived))
    lanes = jnp.arange(rank, dtype=jnp.int32)
    flags = jnp.sum(
        jnp.where(owners[:, None] == lanes[None, :], inside[:, None], 0).astype(jnp.float32), axis=0
    )
    message = jnp.concatenate(
        [jnp.sum(arrived, axis=0), jnp.broadcast_to(flags[None, :], (share, rank))], axis=0
    )
    spread_out = spread(message, n_wide, "wide")
    second_part = run_pass(
        pass_two_kernel, 1, 2, tables, local_blocks, a_all, factor_c, n_wide, True, second_part
    )
    second_part, spread_out = lax.optimization_barrier((second_part, spread_out))
    gram_a = spread_out[:, :share].reshape(rank, rank)
    scale_b = unit_scale(gram_a, gram_c)
    wire = (second_part * (scale_b * WIRE_SCALE)[None]).astype(jnp.float16)
    received_b = exchange(wire, "wide").astype(jnp.float32)
    flags_abs = jnp.sum(
        jnp.where(lanes[None, :] == w, spread_out[:, share], 0.0), axis=1
    ).astype(jnp.int32)
    factors_b = invert(gram_a, gram_c, scale_b)
    vmem = pl.BlockSpec(memory_space=pltpu.VMEM)
    b_new = pl.pallas_call(
        apply_second_kernel,
        out_shape=out,
        in_specs=[pl.BlockSpec(memory_space=pltpu.SMEM)] + [vmem] * 5,
        out_specs=vmem,
        scratch_shapes=[pltpu.VMEM((TJ_DEV, bs, rank), jnp.float32)],
    )(flags_abs, received_b, *factors_b)
    return (a_new, b_new)


def solution(mesh):
    return jax.shard_map(
        local,
        mesh=mesh,
        in_specs=(
            P("wide", "narrow", None, None, None),
            P("wide", "narrow", None),
            P("wide", "narrow", None),
            P("wide", "narrow", None),
            P("wide", "narrow"),
            P(("wide", "narrow"), None),
            P(),
        ),
        out_specs=(P(("wide", "narrow"), None), P(("wide", "narrow"), None)),
        check_vma=False,
    )
```

profile of v0, /device:TPU:1, one launch (start us, length us, event | category | flops | bytes accessed | tf_op | source)
XLA Modules:
  0.0 188.4 jit_solution(14798704363903517290)
XLA Ops:
  0.6 2.1 %collective-permute-start = (bf16[1,128,256]{2,1,0:T(8,128)(2,1)}, bf16[1,128,256]{2,1,0:T(8,128)(2,1)S(1)}, u32[]{:S(2)}, u32[]{:S(2)}) collective-permute-start(bf16[1,128,256]{2,1,0:T(8,128)(2,1)} %bitcast.76), channel_id=1, source_target_pairs={{0,64},{8,72},{16,80},{24,88},{32,96},{40,104},{48,112},{56,120},{... | collective-permute-start | bytes 196616 | tf_op jit(solution)/shard_map/ppermute | solution.py:33
  2.7 2.5 %collective-permute-start.1 = (bf16[1,128,256]{2,1,0:T(8,128)(2,1)}, bf16[1,128,256]{2,1,0:T(8,128)(2,1)S(1)}, u32[]{:S(2)}, u32[]{:S(2)}) collective-permute-start(bf16[1,128,256]{2,1,0:T(8,128)(2,1)} %bitcast.77), channel_id=1, source_target_pairs={{0,128},{8,136},{16,144},{24,152},{32,160},{40,168},{48,176},{56,1... | collective-permute-start | bytes 196616 | tf_op jit(solution)/shard_map/ppermute | solution.py:33
  5.2 1.2 collective-permute-start.2
  6.3 1.5 constant_dynamic-update-slice_fusion.6
  8.0 0.8 collective-permute-done.2
  8.8 0.9 pad_maximum_fusion
  9.7 1.6 collective-permute-start.3
  11.3 2.6 %collective-permute-start.4 = (bf16[4,128,256]{2,1,0:T(8,128)(2,1)S(1)}, bf16[4,128,256]{2,1,0:T(8,128)(2,1)S(1)}, u32[]{:S(2)}, u32[]{:S(2)}) collective-permute-start(bf16[4,128,256]{2,1,0:T(8,128)(2,1)S(1)} %pad_maximum_fusion), channel_id=1, source_target_pairs={{0,32},{8,40},{16,48},{24,56},{32,0},{40,8},{48,16},{56,24},{64,96... | collective-permute-start | bytes 786440 | tf_op jit(solution)/shard_map/ppermute | solution.py:33
  13.9 1.1 collective-permute-start.5
  17.1 0.7 constant_dynamic-update-slice_fusion.2
  17.8 6.2 %collective-permute-done.4 = bf16[4,128,256]{2,1,0:T(8,128)(2,1)S(1)} collective-permute-done((bf16[4,128,256]{2,1,0:T(8,128)(2,1)S(1)}, bf16[4,128,256]{2,1,0:T(8,128)(2,1)S(1)}, u32[]{:S(2)}, u32[]{:S(2)}) %collective-permute-start.4) | collective-permute-done | bytes 262176 | tf_op jit(solution)/shard_map/ppermute | solution.py:33
  24.8 0.8 constant_dynamic-update-slice_fusion
  25.6 2.7 %collective-permute-start.6 = (bf16[16,128,256]{2,1,0:T(8,128)(2,1)}, bf16[16,128,256]{2,1,0:T(8,128)(2,1)S(1)}, u32[]{:S(2)}, u32[]{:S(2)}) collective-permute-start(bf16[16,128,256]{2,1,0:T(8,128)(2,1)} %get-tuple-element.37), channel_id=1, source_target_pairs={{0,8},{8,0},{16,24},{24,16},{32,40},{40,32},{48,56},{56,48},{64,72... | collective-permute-start | bytes 3145736 | tf_op jit(solution)/shard_map/ppermute | solution.py:33
  28.3 2.5 %collective-permute-done.6 = bf16[16,128,256]{2,1,0:T(8,128)(2,1)S(1)} collective-permute-done((bf16[16,128,256]{2,1,0:T(8,128)(2,1)}, bf16[16,128,256]{2,1,0:T(8,128)(2,1)S(1)}, u32[]{:S(2)}, u32[]{:S(2)}) %collective-permute-start.6) | collective-permute-done | bytes 1048608 | tf_op jit(solution)/shard_map/ppermute | solution.py:33
  30.9 0.7 convolution_bitcast_fusion
  33.0 8.2 %all-to-all-start = ((f32[8,32,256]{2,1,0:T(8,128)}), f32[8,32,256]{2,1,0:T(8,128)S(1)}, u32[]{:S(2)}, u32[]{:S(2)}) async-start(f32[8,32,256]{2,1,0:T(8,128)} %broadcast_in_dim.34), calls=%async_computation | async-start | bytes 524288 | tf_op jit(solution)/shard_map/all_to_all | solution.py:242
  42.4 10.0 %shard_map.86 = f32[16,64,256]{2,1,0:T(8,128)} custom-call(s32[16]{0:T(128)} %bitcast.87, s32[16]{0:T(128)} %get-tuple-element.30.picks_ref, s32[16]{0:T(128)} %bitcast.80, s32[1]{0:T(128)} %bitcast.67.count_ref, bf16[16,64,4096]{2,1,0:T(8,128)(2,1)} %bitcast.70, bf16[1024,256]{1,0:T(8,128)(2,1)} %c_ref.5, bf16[32,128,256]{2,1,0:T(8,128)(2,1)} %copy-done.2, ...), custom_call_target="tpu_custom_call" | custom-call | flops 2147483648 | bytes 8388608 | tf_op jit(solution)/shard_map/pallas_call | solution.py:110
  52.5 2.0 %collective-permute-start.7 = (f32[32,256]{1,0:T(8,128)S(1)}, f32[32,256]{1,0:T(8,128)S(1)}, u32[]{:S(2)}, u32[]{:S(2)}) collective-permute-start(f32[32,256]{1,0:T(8,128)S(1)} %reduce_sum.54), channel_id=1, source_target_pairs={{0,192},{8,200},{16,208},{24,216},{32,224},{40,232},{48,240},{56,2... | collective-permute-start | bytes 98312 | tf_op jit(solution)/shard_map/ppermute | solution.py:33
  54.5 3.7 %collective-permute-start.8 = (f32[32,256]{1,0:T(8,128)S(1)}, f32[32,256]{1,0:T(8,128)S(1)}, u32[]{:S(2)}, u32[]{:S(2)}) collective-permute-start(f32[32,256]{1,0:T(8,128)S(1)} %reduce_sum.54), channel_id=1, source_target_pairs={{0,128},{8,136},{16,144},{24,152},{32,160},{40,168},{48,176},{56,1... | collective-permute-start | bytes 98312 | tf_op jit(solution)/shard_map/ppermute | solution.py:33
  58.9 7.1 %all-to-all-start.1 = ((f32[8,128,256]{2,1,0:T(8,128)}), f32[8,128,256]{2,1,0:T(8,128)S(1)}, u32[]{:S(2)}, u32[]{:S(2)}) async-start(f32[8,128,256]{2,1,0:T(8,128)} %bitcast.75), calls=%async_computation.1 | async-start | bytes 2097152 | tf_op jit(solution)/shard_map/all_to_all | solution.py:242
  66.1 1.6 collective-permute-start.10
  67.7 1.0 collective-permute-done.10
  68.8 1.1 pad_maximum_fusion.1
  70.4 9.5 %shard_map.87 = (f32[128,128]{1,0:T(8,128)}, f32[128,128]{1,0:T(8,128)}, f32[128,128]{1,0:T(8,128)}) custom-call(f32[256,256]{1,0:T(8,128)} %get-tuple-element.33.g_ref, f32[256,256]{1,0:T(8,128)} %get-tuple-element.53.c_ref, f32[1,256]{1,0:T(1,128)} %bitcast.85), custom_call_target="tpu_custom_call" | custom-call | flops 10000000000 | bytes 1000000 | tf_op jit(solution)/shard_map/pallas_call | solution.py:204
  79.8 15.3 %all-to-all-done.1.m_ref = f32[8,128,256]{2,1,0:T(8,128)S(1)} async-done(((f32[8,128,256]{2,1,0:T(8,128)}), f32[8,128,256]{2,1,0:T(8,128)S(1)}, u32[]{:S(2)}, u32[]{:S(2)}) %all-to-all-start.1) | async-done | bytes 1048608 | tf_op jit(solution)/shard_map/all_to_all | solution.py:242
  95.2 1.0 copy-done.3
  96.1 2.6 %shard_map.88 = (f32[128,256]{1,0:T(8,128)}, bf16[128,256]{1,0:T(8,128)(2,1)}) custom-call(f32[8,128,256]{2,1,0:T(8,128)} %copy-done.3, f32[1,256]{1,0:T(1,128)} %bitcast.86, f32[128,128]{1,0:T(8,128)} %get-tuple-element.18.a1_ref, f32[128,128]{1,0:T(8,128)} %get-tuple-element.19.t_ref, f32[128,128]{1,0:T(8,128)} %get-tuple-element.20.s1_ref), custom_call_target="tpu_custom_call" | custom-call | tf_op jit(solution)/shard_map/pallas_call | solution.py:312
  98.8 0.9 constant_dynamic-update-slice_fusion.30
  99.7 1.9 %collective-permute-start.13 = (bf16[128,256]{1,0:T(8,128)(2,1)}, bf16[128,256]{1,0:T(8,128)(2,1)S(1)}, u32[]{:S(2)}, u32[]{:S(2)}) collective-permute-start(bf16[128,256]{1,0:T(8,128)(2,1)} %get-tuple-element.22), channel_id=1, source_target_pairs={{0,3},{1,4},{2,5},{3,6},{4,7},{5,0},{6,1},{7,2},{8,11},{9,12},{10,... | collective-permute-start | bytes 196616 | tf_op jit(solution)/shard_map/ppermute | solution.py:319
  101.6 3.7 %collective-permute-start.14 = (bf16[128,256]{1,0:T(8,128)(2,1)}, bf16[128,256]{1,0:T(8,128)(2,1)S(1)}, u32[]{:S(2)}, u32[]{:S(2)}) collective-permute-start(bf16[128,256]{1,0:T(8,128)(2,1)} %get-tuple-element.22), channel_id=1, source_target_pairs={{0,4},{1,5},{2,6},{3,7},{4,0},{5,1},{6,2},{7,3},{8,12},{9,13},{10,... | collective-permute-start | bytes 196616 | tf_op jit(solution)/shard_map/ppermute | solution.py:319
  105.8 3.1 %collective-permute-start.16 = (bf16[128,256]{1,0:T(8,128)(2,1)}, bf16[128,256]{1,0:T(8,128)(2,1)S(1)}, u32[]{:S(2)}, u32[]{:S(2)}) collective-permute-start(bf16[128,256]{1,0:T(8,128)(2,1)} %get-tuple-element.22), channel_id=1, source_target_pairs={{0,6},{1,7},{2,0},{3,1},{4,2},{5,3},{6,4},{7,5},{8,14},{9,15},{10,... | collective-permute-start | bytes 196616 | tf_op jit(solution)/shard_map/ppermute | solution.py:319
  109.3 1.2 collective-permute-done.14
  110.5 3.0 %collective-permute-done.15 = bf16[128,256]{1,0:T(8,128)(2,1)S(1)} collective-permute-done((bf16[128,256]{1,0:T(8,128)(2,1)}, bf16[128,256]{1,0:T(8,128)(2,1)S(1)}, u32[]{:S(2)}, u32[]{:S(2)}) %collective-permute-start.15) | collective-permute-done | bytes 65568 | tf_op jit(solution)/shard_map/ppermute | solution.py:319
  113.5 3.5 %collective-permute-done.16 = bf16[128,256]{1,0:T(8,128)(2,1)S(1)} collective-permute-done((bf16[128,256]{1,0:T(8,128)(2,1)}, bf16[128,256]{1,0:T(8,128)(2,1)S(1)}, u32[]{:S(2)}, u32[]{:S(2)}) %collective-permute-start.16) | collective-permute-done | bytes 65568 | tf_op jit(solution)/shard_map/ppermute | solution.py:319
  117.0 1.9 %collective-permute-done.17 = bf16[128,256]{1,0:T(8,128)(2,1)S(1)} collective-permute-done((bf16[128,256]{1,0:T(8,128)(2,1)}, bf16[128,256]{1,0:T(8,128)(2,1)S(1)}, u32[]{:S(2)}, u32[]{:S(2)}) %collective-permute-start.17) | collective-permute-done | bytes 65568 | tf_op jit(solution)/shard_map/ppermute | solution.py:319
  119.2 1.0 fusion
  120.2 7.3 %all-to-all-start.2 = ((f32[32,8,256]{2,1,0:T(8,128)}), f32[32,8,256]{2,1,0:T(8,128)S(1)}, u32[]{:S(2)}, u32[]{:S(2)}) async-start(f32[32,8,256]{2,1,0:T(8,128)} %fusion), calls=%async_computation.2 | async-start | bytes 524288 | tf_op jit(solution)/shard_map/all_to_all | solution.py:242
  128.1 9.9 %shard_map.89.rest_2_ = f32[32,64,256]{2,1,0:T(8,128)} custom-call(s32[16]{0:T(128)} %fusion.5.picks_ref, s32[16]{0:T(128)} %copy-done.5, s32[16]{0:T(128)} %bitcast.81, s32[1]{0:T(128)} %bitcast.68.count_ref, bf16[16,64,4096]{2,1,0:T(8,128)(2,1)} %bitcast.71, bf16[1024,256]{1,0:T(8,128)(2,1)} %c_ref.5, bf16[8,128,256]{2,1,0:T(8,128)(2,1)} %copy-done, ...), custom_call_target="tpu_custom_call" | custom-call | flops 1073741824 | bytes 4194304 | tf_op jit(solution)/shard_map/pallas_call | solution.py:110
  138.1 0.9 broadcast_in_dim.68
  138.9 7.4 %all-to-all-start.3 = ((f32[32,16,256]{2,1,0:T(8,128)}), f32[32,16,256]{2,1,0:T(8,128)S(1)}, u32[]{:S(2)}, u32[]{:S(2)}) async-start(f32[32,16,256]{2,1,0:T(8,128)} %broadcast_in_dim.68), calls=%async_computation.3 | async-start | bytes 1048576 | tf_op jit(solution)/shard_map/all_to_all | solution.py:242
  146.3 4.9 %shard_map.90 = f32[32,64,256]{2,1,0:T(8,128)} custom-call(s32[16]{0:T(128)} %fusion.5.picks_ref, s32[16]{0:T(128)} %copy-done.5, s32[16]{0:T(128)} %bitcast.82, s32[1]{0:T(128)} %bitcast.69.count_ref, bf16[16,64,4096]{2,1,0:T(8,128)(2,1)} %bitcast.72, bf16[1024,256]{1,0:T(8,128)(2,1)} %c_ref.5, bf16[8,128,256]{2,1,0:T(8,128)(2,1)} %copy-done, ...), custom_call_target="tpu_custom_call" | custom-call | flops 1073741824 | bytes 4194304 | tf_op jit(solution)/shard_map/pallas_call | solution.py:110
  151.2 6.7 %all-to-all-done.3 = f32[32,16,256]{2,1,0:T(8,128)S(1)} async-done(((f32[32,16,256]{2,1,0:T(8,128)}), f32[32,16,256]{2,1,0:T(8,128)S(1)}, u32[]{:S(2)}, u32[]{:S(2)}) %all-to-all-start.3) | async-done | bytes 524320 | tf_op jit(solution)/shard_map/all_to_all | solution.py:242
  159.3 2.9 %multiply_convert_fusion = f16[32,64,256]{2,1,0:T(8,128)(2,1)} fusion(f32[32,64,256]{2,1,0:T(8,128)} %shard_map.90, f32[256]{0:T(256)S(1)} %get-tuple-element.52), kind=kLoop, calls=%fused_computation | loop fusion | flops 1048576 | bytes 3146752 | tf_op jit(solution)/shard_map/convert_element_type | solution.py:346
  162.2 4.4 %all-to-all-start.4 = ((f16[32,64,256]{2,1,0:T(8,128)(2,1)}), f16[32,64,256]{2,1,0:T(8,128)(2,1)S(1)}, u32[]{:S(2)}, u32[]{:S(2)}) async-start(f16[32,64,256]{2,1,0:T(8,128)(2,1)} %multiply_convert_fusion), calls=%async_computation.4 | async-start | bytes 2097152 | tf_op jit(solution)/shard_map/all_to_all | solution.py:242
  167.2 9.5 %shard_map.91 = (f32[128,128]{1,0:T(8,128)}, f32[128,128]{1,0:T(8,128)}, f32[128,128]{1,0:T(8,128)}) custom-call(f32[256,256]{1,0:T(8,128)} %slice_bitcast_fusion.g_ref, f32[256,256]{1,0:T(8,128)} %get-tuple-element.53.c_ref, f32[1,256]{1,0:T(1,128)} %bitcast.83), custom_call_target="tpu_custom_call" | custom-call | flops 10000000000 | bytes 1000000 | tf_op jit(solution)/shard_map/pallas_call | solution.py:204
  176.7 6.8 %all-to-all-done.4 = f16[32,64,256]{2,1,0:T(8,128)(2,1)S(1)} async-done(((f16[32,64,256]{2,1,0:T(8,128)(2,1)}), f16[32,64,256]{2,1,0:T(8,128)(2,1)S(1)}, u32[]{:S(2)}, u32[]{:S(2)}) %all-to-all-start.4) | async-done | bytes 1048608 | tf_op jit(solution)/shard_map/all_to_all | solution.py:242
  183.5 1.6 convert_element_type.15.m_ref
  185.0 3.4 %shard_map.92 = f32[128,256]{1,0:T(8,128)} custom-call(s32[32]{0:T(128)} %convert_element_type.13.flags_ref, f32[32,64,256]{2,1,0:T(8,128)} %convert_element_type.15.m_ref, f32[1,256]{1,0:T(1,128)} %bitcast.84, f32[128,128]{1,0:T(8,128)} %get-tuple-element.27.a1_ref, f32[128,128]{1,0:T(8,128)} %get-tuple-element.28.t_ref, f32[128,128]{1,0:T(8,128)} %get-tuple-element.29.s1_ref), custom_call_target="tpu_custom_call" | custom-call | tf_op jit(solution)/shard_map/pallas_call | solution.py:353
  (72 shorter events, 10.2 us)
Async XLA Ops:
  0.6 7.2 %collective-permute-start = (bf16[1,128,256]{2,1,0:T(8,128)(2,1)}, bf16[1,128,256]{2,1,0:T(8,128)(2,1)S(1)}, u32[]{:S(2)}, u32[]{:S(2)}) collective-permute-start(bf16[1,128,256]{2,1,0:T(8,128)(2,1)} %bitcast.76), channel_id=1, source_target_pairs={{0,64},{8,72},{16,80},{24,88},{32,96},{40,104},{48,112},{56,120},{... | collective-permute-start | bytes 196616 | tf_op jit(solution)/shard_map/ppermute | solution.py:33
  2.7 5.3 %collective-permute-start.1 = (bf16[1,128,256]{2,1,0:T(8,128)(2,1)}, bf16[1,128,256]{2,1,0:T(8,128)(2,1)S(1)}, u32[]{:S(2)}, u32[]{:S(2)}) collective-permute-start(bf16[1,128,256]{2,1,0:T(8,128)(2,1)} %bitcast.77), channel_id=1, source_target_pairs={{0,128},{8,136},{16,144},{24,152},{32,160},{40,168},{48,176},{56,1... | collective-permute-start | bytes 196616 | tf_op jit(solution)/shard_map/ppermute | solution.py:33
  5.2 3.6 %collective-permute-start.2 = (bf16[1,128,256]{2,1,0:T(8,128)(2,1)}, bf16[1,128,256]{2,1,0:T(8,128)(2,1)S(1)}, u32[]{:S(2)}, u32[]{:S(2)}) collective-permute-start(bf16[1,128,256]{2,1,0:T(8,128)(2,1)} %bitcast.78), channel_id=1, source_target_pairs={{0,192},{8,200},{16,208},{24,216},{32,224},{40,232},{48,240},{56,2... | collective-permute-start | bytes 196616 | tf_op jit(solution)/shard_map/ppermute | solution.py:33
  9.7 7.4 %collective-permute-start.3 = (bf16[4,128,256]{2,1,0:T(8,128)(2,1)S(1)}, bf16[4,128,256]{2,1,0:T(8,128)(2,1)S(1)}, u32[]{:S(2)}, u32[]{:S(2)}) collective-permute-start(bf16[4,128,256]{2,1,0:T(8,128)(2,1)S(1)} %pad_maximum_fusion), channel_id=1, source_target_pairs={{0,16},{8,24},{16,32},{24,40},{32,48},{40,56},{48,0},{56,8},{64,80... | collective-permute-start | bytes 786440 | tf_op jit(solution)/shard_map/ppermute | solution.py:33
  11.3 12.8 %collective-permute-start.4 = (bf16[4,128,256]{2,1,0:T(8,128)(2,1)S(1)}, bf16[4,128,256]{2,1,0:T(8,128)(2,1)S(1)}, u32[]{:S(2)}, u32[]{:S(2)}) collective-permute-start(bf16[4,128,256]{2,1,0:T(8,128)(2,1)S(1)} %pad_maximum_fusion), channel_id=1, source_target_pairs={{0,32},{8,40},{16,48},{24,56},{32,0},{40,8},{48,16},{56,24},{64,96... | collective-permute-start | bytes 786440 | tf_op jit(solution)/shard_map/ppermute | solution.py:33
  13.9 10.9 %collective-permute-start.5 = (bf16[4,128,256]{2,1,0:T(8,128)(2,1)S(1)}, bf16[4,128,256]{2,1,0:T(8,128)(2,1)S(1)}, u32[]{:S(2)}, u32[]{:S(2)}) collective-permute-start(bf16[4,128,256]{2,1,0:T(8,128)(2,1)S(1)} %pad_maximum_fusion), channel_id=1, source_target_pairs={{0,48},{8,56},{16,0},{24,8},{32,16},{40,24},{48,32},{56,40},{64,11... | collective-permute-start | bytes 786440 | tf_op jit(solution)/shard_map/ppermute | solution.py:33
  25.6 5.2 %collective-permute-start.6 = (bf16[16,128,256]{2,1,0:T(8,128)(2,1)}, bf16[16,128,256]{2,1,0:T(8,128)(2,1)S(1)}, u32[]{:S(2)}, u32[]{:S(2)}) collective-permute-start(bf16[16,128,256]{2,1,0:T(8,128)(2,1)} %get-tuple-element.37), channel_id=1, source_target_pairs={{0,8},{8,0},{16,24},{24,16},{32,40},{40,32},{48,56},{56,48},{64,72... | collective-permute-start | bytes 3145736 | tf_op jit(solution)/shard_map/ppermute | solution.py:33
  30.9 1.4 copy-start.2
  30.9 10.9 %copy-start.7 = (s32[1,1,16]{2,1,0:T(1,128)S(1)}, s32[1,1,16]{2,1,0:T(1,128)}, u32[]{:S(2)}) copy-start(s32[1,1,16]{2,1,0:T(1,128)} %param.9) | copy-start | bytes 196
  33.0 19.4 %all-to-all-start = ((f32[8,32,256]{2,1,0:T(8,128)}), f32[8,32,256]{2,1,0:T(8,128)S(1)}, u32[]{:S(2)}, u32[]{:S(2)}) async-start(f32[8,32,256]{2,1,0:T(8,128)} %broadcast_in_dim.34), calls=%async_computation | async-start | bytes 524288 | tf_op jit(solution)/shard_map/all_to_all | solution.py:242
  42.4 85.6 %copy-start.5 = (s32[16]{0:T(128)}, s32[16]{0:T(128)S(1)}, u32[]{:S(2)}) copy-start(s32[16]{0:T(128)S(1)} %get-tuple-element.31.owners_ref) | copy-start | bytes 196
  52.4 16.3 %copy-start.1 = (bf16[1024,256]{1,0:T(8,128)(2,1)S(1)}, bf16[1024,256]{1,0:T(8,128)(2,1)}, u32[]{:S(2)}) copy-start(bf16[1024,256]{1,0:T(8,128)(2,1)} %c_ref.5) | copy-start | bytes 1572868
  52.5 13.5 %collective-permute-start.7 = (f32[32,256]{1,0:T(8,128)S(1)}, f32[32,256]{1,0:T(8,128)S(1)}, u32[]{:S(2)}, u32[]{:S(2)}) collective-permute-start(f32[32,256]{1,0:T(8,128)S(1)} %reduce_sum.54), channel_id=1, source_target_pairs={{0,192},{8,200},{16,208},{24,216},{32,224},{40,232},{48,240},{56,2... | collective-permute-start | bytes 98312 | tf_op jit(solution)/shard_map/ppermute | solution.py:33
  54.5 11.5 %collective-permute-start.8 = (f32[32,256]{1,0:T(8,128)S(1)}, f32[32,256]{1,0:T(8,128)S(1)}, u32[]{:S(2)}, u32[]{:S(2)}) collective-permute-start(f32[32,256]{1,0:T(8,128)S(1)} %reduce_sum.54), channel_id=1, source_target_pairs={{0,128},{8,136},{16,144},{24,152},{32,160},{40,168},{48,176},{56,1... | collective-permute-start | bytes 98312 | tf_op jit(solution)/shard_map/ppermute | solution.py:33
  58.2 7.8 %collective-permute-start.9 = (f32[32,256]{1,0:T(8,128)S(1)}, f32[32,256]{1,0:T(8,128)S(1)}, u32[]{:S(2)}, u32[]{:S(2)}) collective-permute-start(f32[32,256]{1,0:T(8,128)S(1)} %reduce_sum.54), channel_id=1, source_target_pairs={{0,64},{8,72},{16,80},{24,88},{32,96},{40,104},{48,112},{56,120},{... | collective-permute-start | bytes 98312 | tf_op jit(solution)/shard_map/ppermute | solution.py:33
  58.9 36.2 %all-to-all-start.1 = ((f32[8,128,256]{2,1,0:T(8,128)}), f32[8,128,256]{2,1,0:T(8,128)S(1)}, u32[]{:S(2)}, u32[]{:S(2)}) async-start(f32[8,128,256]{2,1,0:T(8,128)} %bitcast.75), calls=%async_computation.1 | async-start | bytes 2097152 | tf_op jit(solution)/shard_map/all_to_all | solution.py:242
  66.1 2.6 %collective-permute-start.10 = (f32[128,256]{1,0:T(8,128)S(1)}, f32[128,256]{1,0:T(8,128)S(1)}, u32[]{:S(2)}, u32[]{:S(2)}) collective-permute-start(f32[128,256]{1,0:T(8,128)S(1)} %constant_dynamic-slice_fusion), channel_id=1, source_target_pairs={{0,8},{8,0},{16,24},{24,16},{32,40},{40,32},{48,56},{56,48},{64,72... | collective-permute-start | bytes 393224 | tf_op jit(solution)/shard_map/ppermute | solution.py:33
  95.2 1.0 copy-start.3
  98.8 28.7 %copy-start.6 = (s32[1,1,16]{2,1,0:T(1,128)S(1)}, s32[1,1,16]{2,1,0:T(1,128)}, u32[]{:S(2)}) copy-start(s32[1,1,16]{2,1,0:T(1,128)} %param.8) | copy-start | bytes 196
  98.8 7.0 %collective-permute-start.11 = (bf16[128,256]{1,0:T(8,128)(2,1)}, bf16[128,256]{1,0:T(8,128)(2,1)S(1)}, u32[]{:S(2)}, u32[]{:S(2)}) collective-permute-start(bf16[128,256]{1,0:T(8,128)(2,1)} %get-tuple-element.22), channel_id=1, source_target_pairs={{0,1},{1,2},{2,3},{3,4},{4,5},{5,6},{6,7},{7,0},{8,9},{9,10},{10,1... | collective-permute-start | bytes 196616 | tf_op jit(solution)/shard_map/ppermute | solution.py:319
  99.7 9.2 %collective-permute-start.12 = (bf16[128,256]{1,0:T(8,128)(2,1)}, bf16[128,256]{1,0:T(8,128)(2,1)S(1)}, u32[]{:S(2)}, u32[]{:S(2)}) collective-permute-start(bf16[128,256]{1,0:T(8,128)(2,1)} %get-tuple-element.22), channel_id=1, source_target_pairs={{0,2},{1,3},{2,4},{3,5},{4,6},{5,7},{6,0},{7,1},{8,10},{9,11},{10,... | collective-permute-start | bytes 196616 | tf_op jit(solution)/shard_map/ppermute | solution.py:319
  99.7 9.6 %collective-permute-start.13 = (bf16[128,256]{1,0:T(8,128)(2,1)}, bf16[128,256]{1,0:T(8,128)(2,1)S(1)}, u32[]{:S(2)}, u32[]{:S(2)}) collective-permute-start(bf16[128,256]{1,0:T(8,128)(2,1)} %get-tuple-element.22), channel_id=1, source_target_pairs={{0,3},{1,4},{2,5},{3,6},{4,7},{5,0},{6,1},{7,2},{8,11},{9,12},{10,... | collective-permute-start | bytes 196616 | tf_op jit(solution)/shard_map/ppermute | solution.py:319
  101.6 8.9 %collective-permute-start.14 = (bf16[128,256]{1,0:T(8,128)(2,1)}, bf16[128,256]{1,0:T(8,128)(2,1)S(1)}, u32[]{:S(2)}, u32[]{:S(2)}) collective-permute-start(bf16[128,256]{1,0:T(8,128)(2,1)} %get-tuple-element.22), channel_id=1, source_target_pairs={{0,4},{1,5},{2,6},{3,7},{4,0},{5,1},{6,2},{7,3},{8,12},{9,13},{10,... | collective-permute-start | bytes 196616 | tf_op jit(solution)/shard_map/ppermute | solution.py:319
  105.3 8.2 %collective-permute-start.15 = (bf16[128,256]{1,0:T(8,128)(2,1)}, bf16[128,256]{1,0:T(8,128)(2,1)S(1)}, u32[]{:S(2)}, u32[]{:S(2)}) collective-permute-start(bf16[128,256]{1,0:T(8,128)(2,1)} %get-tuple-element.22), channel_id=1, source_target_pairs={{0,5},{1,6},{2,7},{3,0},{4,1},{5,2},{6,3},{7,4},{8,13},{9,14},{10,... | collective-permute-start | bytes 196616 | tf_op jit(solution)/shard_map/ppermute | solution.py:319
  105.8 11.2 %collective-permute-start.16 = (bf16[128,256]{1,0:T(8,128)(2,1)}, bf16[128,256]{1,0:T(8,128)(2,1)S(1)}, u32[]{:S(2)}, u32[]{:S(2)}) collective-permute-start(bf16[128,256]{1,0:T(8,128)(2,1)} %get-tuple-element.22), channel_id=1, source_target_pairs={{0,6},{1,7},{2,0},{3,1},{4,2},{5,3},{6,4},{7,5},{8,14},{9,15},{10,... | collective-permute-start | bytes 196616 | tf_op jit(solution)/shard_map/ppermute | solution.py:319
  108.9 10.0 %collective-permute-start.17 = (bf16[128,256]{1,0:T(8,128)(2,1)}, bf16[128,256]{1,0:T(8,128)(2,1)S(1)}, u32[]{:S(2)}, u32[]{:S(2)}) collective-permute-start(bf16[128,256]{1,0:T(8,128)(2,1)} %get-tuple-element.22), channel_id=1, source_target_pairs={{0,7},{1,0},{2,1},{3,2},{4,3},{5,4},{6,5},{7,6},{8,15},{9,8},{10,9... | collective-permute-start | bytes 196616 | tf_op jit(solution)/shard_map/ppermute | solution.py:319
  118.9 9.1 %copy-start = (bf16[8,128,256]{2,1,0:T(8,128)(2,1)}, bf16[8,128,256]{2,1,0:T(8,128)(2,1)S(1)}, u32[]{:S(2)}) copy-start(bf16[8,128,256]{2,1,0:T(8,128)(2,1)S(1)} %constant_dynamic-update-slice_fusion.23.rest_0_.rest_1_) | copy-start | bytes 1572868
  120.2 17.8 %all-to-all-start.2 = ((f32[32,8,256]{2,1,0:T(8,128)}), f32[32,8,256]{2,1,0:T(8,128)S(1)}, u32[]{:S(2)}, u32[]{:S(2)}) async-start(f32[32,8,256]{2,1,0:T(8,128)} %fusion), calls=%async_computation.2 | async-start | bytes 524288 | tf_op jit(solution)/shard_map/all_to_all | solution.py:242
  138.9 19.0 %all-to-all-start.3 = ((f32[32,16,256]{2,1,0:T(8,128)}), f32[32,16,256]{2,1,0:T(8,128)S(1)}, u32[]{:S(2)}, u32[]{:S(2)}) async-start(f32[32,16,256]{2,1,0:T(8,128)} %broadcast_in_dim.68), calls=%async_computation.3 | async-start | bytes 1048576 | tf_op jit(solution)/shard_map/all_to_all | solution.py:242
  146.3 12.3 %copy-start.4 = (f32[256,256]{1,0:T(8,128)S(1)}, f32[256,256]{1,0:T(8,128)}, u32[]{:S(2)}) copy-start(f32[256,256]{1,0:T(8,128)} %get-tuple-element.53.c_ref) | copy-start | bytes 786436
  162.2 21.3 %all-to-all-start.4 = ((f16[32,64,256]{2,1,0:T(8,128)(2,1)}), f16[32,64,256]{2,1,0:T(8,128)(2,1)S(1)}, u32[]{:S(2)}, u32[]{:S(2)}) async-start(f16[32,64,256]{2,1,0:T(8,128)(2,1)} %multiply_convert_fusion), calls=%async_computation.4 | async-start | bytes 2097152 | tf_op jit(solution)/shard_map/all_to_all | solution.py:242
where the time goes:
time: 189 us; the launch traced here: 188 us
  starting transfers between devices  65.7 us (35%)
  Pallas kernels  49.8 us (26%)
  waiting for transfers between devices  49.3 us (26%)
  local copies, waits for them, and re-layouts  11.4 us (6%)
  other arithmetic  7.86 us (4%)
  matrix products  2.84 us (2%)
    all_to_all x5, starting transfers between devices, exchange(): return lax.all_to_all(parts, axis, 0, 0, tiled=True)  34.3 us
    all_to_all x5, waiting for transfers between devices, exchange(): return lax.all_to_all(parts, axis, 0, 0, tiled=True)  28.8 us
    pallas_call x3, Pallas kernels, run_pass(): pl.pallas_call(functools.partial(kernel, start * UNROLL), out_shape=jax.S...  24.8 us
    ppermute x11, starting transfers between devices, shift_wide(): return lax.ppermute(v, 'wide', pairs)  21.8 us
    pallas_call x2, Pallas kernels, invert(): pl.pallas_call(invert_kernel, out_shape=(sq, sq, sq), cost_estimate=pl.Co...  18.9 us
    ppermute x11, waiting for transfers between devices, shift_wide(): return lax.ppermute(v, 'wide', pairs)  10.9 us
    ppermute x7, waiting for transfers between devices, local(): lax.ppermute(a_half, 'narrow', [(i, (i + k) % n_narrow) for i in range(n_...  9.61 us
    ppermute x7, starting transfers between devices, local(): lax.ppermute(a_half, 'narrow', [(i, (i + k) % n_narrow) for i in range(n_...  9.6 us
  transfers between devices with their start and end apart: 23, of which 13 were waited for; matrix products, arithmetic and copies ran while one was open for 5% of the time, Pallas kernels for 23%

commit v1 on v0

--- a/solution.py
+++ b/solution.py
@@ -179,7 +179,7 @@
     return lax.rsqrt(jnp.sum(diag, axis=0, keepdims=True))
 
 
-def invert_kernel(g_ref, c_ref, scale_ref, a1_ref, t_ref, s1_ref):
+def invert_kernel(g_ref, c_ref, scale_ref, out_ref, a1_ref, s1_ref):
     rank = g_ref.shape[0]
     half = rank // 2
     eye = (
@@ -193,49 +193,37 @@
     sweep_negated_inverse(a1_ref)
     b = g[half:, :half]
     t = mm(b, a1_ref[...])
-    t_ref[...] = t
     s1_ref[...] = g[half:, half:] - mm(t, b, ((1,), (1,)))
     sweep_negated_inverse(s1_ref)
+    s1 = s1_ref[...]
+    low = mm(s1, t)
+    d1 = d_row[:, :half]
+    d2 = d_row[:, half:]
+    out_ref[:half, :half] = (a1_ref[...] + mm(t, low, ((0,), (0,)))) * d1
+    out_ref[:half, half:] = -mm(t, s1, ((0,), (0,))) * d2
+    out_ref[half:, :half] = -low * d1
+    out_ref[half:, half:] = s1 * d2
 
 
 def invert(gram, gram_c, scale):
-    half = gram.shape[0] // 2
-    sq = jax.ShapeDtypeStruct((half, half), jnp.float32)
-    parts = pl.pallas_call(
+    rank = gram.shape[0]
+    half = rank // 2
+    return pl.pallas_call(
         invert_kernel,
-        out_shape=(sq, sq, sq),
+        out_shape=jax.ShapeDtypeStruct((rank, rank), jnp.float32),
+        scratch_shapes=[pltpu.VMEM((half, half), jnp.float32)] * 2,
         cost_estimate=pl.CostEstimate(flops=10**10, bytes_accessed=10**6, transcendentals=0),
     )(gram, gram_c, scale)
-    return (scale, *parts)
-
-
-def apply_inverse(m, scale_ref, a1_ref, t_ref, s1_ref):
-    half = a1_ref.shape[0]
-    m1 = m[:, :half]
-    z2 = mm(m[:, half:] - mm(m1, t_ref[...], ((1,), (1,))), s1_ref[...])
-    z1 = mm(m1, a1_ref[...]) - mm(z2, t_ref[...])
-    return jnp.concatenate([z1, z2], axis=1) * scale_ref[...]
-
-
-def apply_first_kernel(m_ref, scale_ref, a1_ref, t_ref, s1_ref, out_ref, half_ref):
-    m = m_ref[0]
-    for k in range(1, m_ref.shape[0]):
-        m = m + m_ref[k]
-    z = apply_inverse(m * scale_ref[...], scale_ref, a1_ref, t_ref, s1_ref)
+
+
+def apply_first_kernel(m_ref, scale_ref, inverse_ref, out_ref, half_ref):
+    z = mm(m_ref[...] * scale_ref[...], inverse_ref[...])
     out_ref[...] = z
     half_ref[...] = z.astype(jnp.bfloat16)
 
 
-def apply_second_kernel(flags_ref, m_ref, scale_ref, a1_ref, t_ref, s1_ref, out_ref, acc_ref):
-    acc_ref[...] = jnp.zeros_like(acc_ref)
-
-    def step(k, carry):
-        acc_ref[flags_ref[k]] += m_ref[k]
-        return carry
-
-    lax.fori_loop(0, m_ref.shape[0], step, 0)
-    m = acc_ref[...].reshape(out_ref.shape) * (1.0 / WIRE_SCALE)
-    out_ref[...] = apply_inverse(m, scale_ref, a1_ref, t_ref, s1_ref)
+def apply_second_kernel(m_ref, inverse_ref, out_ref):
+    out_ref[...] = mm(m_ref[...] * (1.0 / WIRE_SCALE), inverse_ref[...])
 
 
 def exchange(parts, axis):
@@ -284,7 +272,10 @@
 
     packed = factor_b[None]
     along_x = jnp.concatenate([packed] + [shift_wide(packed, k, 0, 0) for k in (1, 2, 3)], axis=0)
-    along_y = jnp.concatenate([along_x] + [shift_wide(along_x, 0, k, 0) for k in (1, 2, 3)], axis=0)
+    back = shift_wide(along_x, 0, 1, 0)
+    ahead = shift_wide(along_x, 0, 3, 0)
+    middle = [shift_wide(back[:NX // 2], 0, 1, 0), shift_wide(ahead[NX // 2:], 0, 3, 0)]
+    along_y = jnp.concatenate([along_x, back, *middle, ahead], axis=0)
     gathered = jnp.concatenate([along_y, shift_wide(along_y, 0, 0, 1)], axis=0)
 
     def relative(owner):
@@ -307,19 +298,23 @@
     first_part, arrived = lax.optimization_barrier((first_part, arrived))
     received = exchange(first_part.reshape(n_narrow, TI_DEV * bs, rank), "narrow")
     gram_b = gather_slices(jnp.sum(arrived, axis=0), x, c)
-    factors = invert(gram_b, gram_c, unit_scale(gram_b, gram_c))
+    scale_a = unit_scale(gram_b, gram_c)
+    inverse_a = invert(gram_b, gram_c, scale_a)
     out = jax.ShapeDtypeStruct((rows, rank), jnp.float32)
     a_new, a_half = pl.pallas_call(
         apply_first_kernel, out_shape=(out, jax.ShapeDtypeStruct((rows, rank), jnp.bfloat16))
-    )(received, *factors)
-
-    a_all = jnp.stack(
-        [a_half]
-        + [
-            lax.ppermute(a_half, "narrow", [(i, (i + k) % n_narrow) for i in range(n_narrow)])
-            for k in range(1, n_narrow)
-        ]
-    )
+    )(jnp.sum(received, axis=0), scale_a, inverse_a)
+
+    def shift_narrow(v, k):
+        return lax.ppermute(v, "narrow", [(i, (i + k) % n_narrow) for i in range(n_narrow)])
+
+    back_2, ahead_2 = shift_narrow(a_half, 2), shift_narrow(a_half, -2)
+    back_1, ahead_1 = shift_narrow(a_half, 1), shift_narrow(a_half, -1)
+    back_34 = shift_narrow(jnp.concatenate([back_1, back_2[:bs]], axis=0), 2)
+    ahead_34 = shift_narrow(jnp.concatenate([ahead_1, ahead_2[bs:]], axis=0), -2)
+    a_all = jnp.concatenate(
+        [a_half, back_1, back_2, back_34, ahead_34[rows:], ahead_34[:rows], ahead_2, ahead_1], axis=0
+    ).reshape(n_narrow, rows, rank)
     a_pick = ((n - first_ids // TI_DEV) % n_narrow) * TI_DEV + first_ids % TI_DEV
 
     tables = (a_pick, owners, depth_ids, count)
@@ -345,18 +340,17 @@
     scale_b = unit_scale(gram_a, gram_c)
     wire = (second_part * (scale_b * WIRE_SCALE)[None]).astype(jnp.float16)
     received_b = exchange(wire, "wide").astype(jnp.float32)
-    flags_abs = jnp.sum(
-        jnp.where(lanes[None, :] == w, spread_out[:, share], 0.0), axis=1
-    ).astype(jnp.int32)
-    factors_b = invert(gram_a, gram_c, scale_b)
-    vmem = pl.BlockSpec(memory_space=pltpu.VMEM)
-    b_new = pl.pallas_call(
-        apply_second_kernel,
-        out_shape=out,
-        in_specs=[pl.BlockSpec(memory_space=pltpu.SMEM)] + [vmem] * 5,
-        out_specs=vmem,
-        scratch_shapes=[pltpu.VMEM((TJ_DEV, bs, rank), jnp.float32)],
-    )(flags_abs, received_b, *factors_b)
+    upper = jnp.sum(jnp.where(lanes[None, :] == w, spread_out[:, share], 0.0), axis=1)
+    upper = upper[:, None, None] > 0.5
+    mttkrp_b = jnp.concatenate(
+        [
+            jnp.sum(jnp.where(upper, 0.0, received_b), axis=0),
+            jnp.sum(jnp.where(upper, received_b, 0.0), axis=0),
+        ],
+        axis=0,
+    )
+    inverse_b = invert(gram_a, gram_c, scale_b)
+    b_new = pl.pallas_call(apply_second_kernel, out_shape=out)(mttkrp_b, inverse_b)
     return (a_new, b_new)
 
 

time: 189 us -> 184 us (0.974)
  the two profiles are of different devices: /device:TPU:1 before, /device:TPU:33 now
where the time goes in v1:
time: 184 us; the launch traced here: 183 us
  starting transfers between devices  64.9 us (35%)
  Pallas kernels  53.2 us (29%)
  waiting for transfers between devices  42 us (23%)
  local copies, waits for them, and re-layouts  10.8 us (6%)
  other arithmetic  7.6 us (4%)
  matrix products  2.86 us (2%)
    all_to_all x5, starting transfers between devices, exchange(): return lax.all_to_all(parts, axis, 0, 0, tiled=True)  35.6 us
    pallas_call x3, Pallas kernels, run_pass(): pl.pallas_call(functools.partial(kernel, start * UNROLL), out_shape=jax.S...  29.2 us
    all_to_all x5, waiting for transfers between devices, exchange(): return lax.all_to_all(parts, axis, 0, 0, tiled=True)  21.6 us
    ppermute x12, starting transfers between devices, shift_wide(): return lax.ppermute(v, 'wide', pairs)  21 us
    pallas_call x2, Pallas kernels, invert(): pl.pallas_call(invert_kernel, out_shape=jax.ShapeDtypeStruct((rank, rank)...  20 us
    ppermute x6, waiting for transfers between devices, shift_narrow(): lax.ppermute(v, 'narrow', [(i, (i + k) % n_narrow) for i in range(n_narro...  11.5 us
    ppermute x12, waiting for transfers between devices, shift_wide(): return lax.ppermute(v, 'wide', pairs)  9.01 us
    ppermute x6, starting transfers between devices, shift_narrow(): lax.ppermute(v, 'narrow', [(i, (i + k) % n_narrow) for i in range(n_narro...  8.21 us
  transfers between devices with their start and end apart: 23, of which 14 were waited for; matrix products, arithmetic and copies ran while one was open for 5% of the time, Pallas kernels for 27%

profile of v1, /device:TPU:33, one launch (start us, length us, event | category | flops | bytes accessed | tf_op | source)
XLA Modules:
  0.0 183.0 jit_solution(7666889124704559436)
XLA Ops:
  0.6 1.3 collective-permute-start
  1.9 2.5 %collective-permute-start.1 = (bf16[1,128,256]{2,1,0:T(8,128)(2,1)}, bf16[1,128,256]{2,1,0:T(8,128)(2,1)S(1)}, u32[]{:S(2)}, u32[]{:S(2)}) collective-permute-start(bf16[1,128,256]{2,1,0:T(8,128)(2,1)} %bitcast.59), channel_id=1, source_target_pairs={{0,128},{8,136},{16,144},{24,152},{32,160},{40,168},{48,176},{56,1... | collective-permute-start | bytes 196616 | tf_op jit(solution)/shard_map/ppermute | solution.py:33
  4.4 1.2 collective-permute-start.2
  5.5 1.7 collective-permute-done.1
  7.2 1.0 collective-permute-done.2
  8.2 0.9 pad_maximum_fusion
  9.1 1.4 collective-permute-start.3
  10.5 1.5 constant_dynamic-update-slice_fusion.7
  12.0 1.5 collective-permute-start.5
  14.7 1.9 %collective-permute-done.3 = bf16[4,128,256]{2,1,0:T(8,128)(2,1)S(1)} collective-permute-done((bf16[4,128,256]{2,1,0:T(8,128)(2,1)S(1)}, bf16[4,128,256]{2,1,0:T(8,128)(2,1)S(1)}, u32[]{:S(2)}, u32[]{:S(2)}) %collective-permute-start.3) | collective-permute-done | bytes 262176 | tf_op jit(solution)/shard_map/ppermute | solution.py:33
  17.7 2.8 %collective-permute-start.6 = (bf16[2,128,256]{2,1,0:T(8,128)(2,1)S(1)}, bf16[2,128,256]{2,1,0:T(8,128)(2,1)S(1)}, u32[]{:S(2)}, u32[]{:S(2)}) collective-permute-start(bf16[2,128,256]{2,1,0:T(8,128)(2,1)S(1)} %slice.33), channel_id=1, source_target_pairs={{0,48},{8,56},{16,0},{24,8},{32,16},{40,24},{48,32},{56,40},{64,11... | collective-permute-start | bytes 393224 | tf_op jit(solution)/shard_map/ppermute | solution.py:33
  20.5 0.7 constant_dynamic-update-slice_fusion.3
  23.1 0.7 constant_dynamic-update-slice_fusion
  23.9 3.8 %collective-permute-start.7 = (bf16[16,128,256]{2,1,0:T(8,128)(2,1)}, bf16[16,128,256]{2,1,0:T(8,128)(2,1)S(1)}, u32[]{:S(2)}, u32[]{:S(2)}) collective-permute-start(bf16[16,128,256]{2,1,0:T(8,128)(2,1)} %get-tuple-element.27), channel_id=1, source_target_pairs={{0,8},{8,0},{16,24},{24,16},{32,40},{40,32},{48,56},{56,48},{64,72... | collective-permute-start | bytes 3145736 | tf_op jit(solution)/shard_map/ppermute | solution.py:33
  27.6 2.5 %collective-permute-done.7 = bf16[16,128,256]{2,1,0:T(8,128)(2,1)S(1)} collective-permute-done((bf16[16,128,256]{2,1,0:T(8,128)(2,1)}, bf16[16,128,256]{2,1,0:T(8,128)(2,1)S(1)}, u32[]{:S(2)}, u32[]{:S(2)}) %collective-permute-start.7) | collective-permute-done | bytes 1048608 | tf_op jit(solution)/shard_map/ppermute | solution.py:33
  30.3 0.7 convolution_bitcast_fusion.1
  31.6 0.7 broadcast_in_dim.54
  32.3 8.0 %all-to-all-start = ((f32[8,32,256]{2,1,0:T(8,128)}), f32[8,32,256]{2,1,0:T(8,128)S(1)}, u32[]{:S(2)}, u32[]{:S(2)}) async-start(f32[8,32,256]{2,1,0:T(8,128)} %broadcast_in_dim.54), calls=%async_computation | async-start | bytes 524288 | tf_op jit(solution)/shard_map/all_to_all | solution.py:230
  41.5 12.3 %shard_map.86 = f32[16,64,256]{2,1,0:T(8,128)} custom-call(s32[16]{0:T(128)} %bitcast.68, s32[16]{0:T(128)} %get-tuple-element.20.picks_ref, s32[16]{0:T(128)} %bitcast.62, s32[1]{0:T(128)} %bitcast.47.count_ref, bf16[16,64,4096]{2,1,0:T(8,128)(2,1)} %bitcast.50, bf16[1024,256]{1,0:T(8,128)(2,1)} %c_ref.5, bf16[32,128,256]{2,1,0:T(8,128)(2,1)} %copy-done.2, ...), custom_call_target="tpu_custom_call" | custom-call | flops 2147483648 | bytes 8388608 | tf_op jit(solution)/shard_map/pallas_call | solution.py:110
  53.9 4.7 %collective-permute-start.9 = (f32[32,256]{1,0:T(8,128)S(1)}, f32[32,256]{1,0:T(8,128)S(1)}, u32[]{:S(2)}, u32[]{:S(2)}) collective-permute-start(f32[32,256]{1,0:T(8,128)S(1)} %reduce_sum.82), channel_id=1, source_target_pairs={{0,128},{8,136},{16,144},{24,152},{32,160},{40,168},{48,176},{56,1... | collective-permute-start | bytes 98312 | tf_op jit(solution)/shard_map/ppermute | solution.py:33
  58.7 6.6 %all-to-all-start.1 = ((f32[8,128,256]{2,1,0:T(8,128)}), f32[8,128,256]{2,1,0:T(8,128)S(1)}, u32[]{:S(2)}, u32[]{:S(2)}) async-start(f32[8,128,256]{2,1,0:T(8,128)} %bitcast.57), calls=%async_computation.1 | async-start | bytes 2097152 | tf_op jit(solution)/shard_map/all_to_all | solution.py:230
  65.5 1.8 %collective-permute-start.11 = (f32[128,256]{1,0:T(8,128)S(1)}, f32[128,256]{1,0:T(8,128)S(1)}, u32[]{:S(2)}, u32[]{:S(2)}) collective-permute-start(f32[128,256]{1,0:T(8,128)S(1)} %constant_dynamic-slice_fusion), channel_id=1, source_target_pairs={{0,8},{8,0},{16,24},{24,16},{32,40},{40,32},{48,56},{56,48},{64,72... | collective-permute-start | bytes 393224 | tf_op jit(solution)/shard_map/ppermute | solution.py:33
  67.3 1.0 collective-permute-done.11
  68.3 1.1 pad_maximum_fusion.1
  70.0 10.0 %shard_map.87.inverse_ref = f32[256,256]{1,0:T(8,128)} custom-call(f32[256,256]{1,0:T(8,128)} %get-tuple-element.23.g_ref, f32[256,256]{1,0:T(8,128)} %get-tuple-element.45.c_ref, f32[1,256]{1,0:T(1,128)} %bitcast.65), custom_call_target="tpu_custom_call" | custom-call | flops 10000000000 | bytes 1000000 | tf_op jit(solution)/shard_map/pallas_call | solution.py:211
  80.0 10.3 %all-to-all-done.1 = f32[8,128,256]{2,1,0:T(8,128)S(1)} async-done(((f32[8,128,256]{2,1,0:T(8,128)}), f32[8,128,256]{2,1,0:T(8,128)S(1)}, u32[]{:S(2)}, u32[]{:S(2)}) %all-to-all-start.1) | async-done | bytes 1048608 | tf_op jit(solution)/shard_map/all_to_all | solution.py:230
  90.2 0.7 reduce_sum.81.m_ref
  91.0 2.0 %shard_map.88 = (f32[128,256]{1,0:T(8,128)}, bf16[128,256]{1,0:T(8,128)(2,1)}) custom-call(f32[128,256]{1,0:T(8,128)} %reduce_sum.81.m_ref, f32[1,256]{1,0:T(1,128)} %bitcast.66, f32[256,256]{1,0:T(8,128)} %shard_map.87.inverse_ref), custom_call_target="tpu_custom_call" | custom-call | tf_op jit(solution)/shard_map/pallas_call | solution.py:304
  92.9 4.3 %collective-permute-start.15 = (bf16[128,256]{1,0:T(8,128)(2,1)}, bf16[128,256]{1,0:T(8,128)(2,1)S(1)}, u32[]{:S(2)}, u32[]{:S(2)}) collective-permute-start(bf16[128,256]{1,0:T(8,128)(2,1)} %get-tuple-element.13), channel_id=1, source_target_pairs={{0,7},{1,0},{2,1},{3,2},{4,3},{5,4},{6,5},{7,6},{8,15},{9,8},{10,9... | collective-permute-start | bytes 196616 | tf_op jit(solution)/shard_map/ppermute | solution.py:309
  97.2 2.4 %collective-permute-start.13 = (bf16[128,256]{1,0:T(8,128)(2,1)}, bf16[128,256]{1,0:T(8,128)(2,1)S(1)}, u32[]{:S(2)}, u32[]{:S(2)}) collective-permute-start(bf16[128,256]{1,0:T(8,128)(2,1)} %get-tuple-element.13), channel_id=1, source_target_pairs={{0,2},{1,3},{2,4},{3,5},{4,6},{5,7},{6,0},{7,1},{8,10},{9,11},{10,... | collective-permute-start | bytes 196616 | tf_op jit(solution)/shard_map/ppermute | solution.py:309
  99.6 0.9 constant_dynamic-update-slice_fusion.32
  100.5 1.6 collective-permute-done.15
  102.1 1.5 collective-permute-start.17
  103.6 1.7 collective-permute-done.12
  105.4 8.2 %collective-permute-done.14 = bf16[192,256]{1,0:T(8,128)(2,1)S(1)} collective-permute-done((bf16[192,256]{1,0:T(8,128)(2,1)S(1)}, bf16[192,256]{1,0:T(8,128)(2,1)S(1)}, u32[]{:S(2)}, u32[]{:S(2)}) %collective-permute-start.14) | collective-permute-done | bytes 98336 | tf_op jit(solution)/shard_map/ppermute | solution.py:309
  113.7 1.1 convolution_bitcast_fusion
  114.7 8.3 %all-to-all-start.2 = ((f32[32,8,256]{2,1,0:T(8,128)}), f32[32,8,256]{2,1,0:T(8,128)S(1)}, u32[]{:S(2)}, u32[]{:S(2)}) async-start(f32[32,8,256]{2,1,0:T(8,128)} %convolution_bitcast_fusion), calls=%async_computation.2 | async-start | bytes 524288 | tf_op jit(solution)/shard_map/all_to_all | solution.py:230
  123.6 9.9 %shard_map.89.rest_2_ = f32[32,64,256]{2,1,0:T(8,128)} custom-call(s32[16]{0:T(128)} %fusion.5.picks_ref, s32[16]{0:T(128)} %copy-done.4, s32[16]{0:T(128)} %bitcast.63, s32[1]{0:T(128)} %bitcast.48.count_ref, bf16[16,64,4096]{2,1,0:T(8,128)(2,1)} %bitcast.51, bf16[1024,256]{1,0:T(8,128)(2,1)} %c_ref.5, bf16[8,128,256]{2,1,0:T(8,128)(2,1)} %bitcast.53, ...), custom_call_target="tpu_custom_call" | custom-call | flops 1073741824 | bytes 4194304 | tf_op jit(solution)/shard_map/pallas_call | solution.py:110
  133.6 0.9 broadcast_in_dim.89
  134.4 7.4 %all-to-all-start.3 = ((f32[32,16,256]{2,1,0:T(8,128)}), f32[32,16,256]{2,1,0:T(8,128)S(1)}, u32[]{:S(2)}, u32[]{:S(2)}) async-start(f32[32,16,256]{2,1,0:T(8,128)} %broadcast_in_dim.89), calls=%async_computation.3 | async-start | bytes 1048576 | tf_op jit(solution)/shard_map/all_to_all | solution.py:230
  141.8 7.1 %shard_map.90 = f32[32,64,256]{2,1,0:T(8,128)} custom-call(s32[16]{0:T(128)} %fusion.5.picks_ref, s32[16]{0:T(128)} %copy-done.4, s32[16]{0:T(128)} %bitcast.64, s32[1]{0:T(128)} %bitcast.49.count_ref, bf16[16,64,4096]{2,1,0:T(8,128)(2,1)} %bitcast.52, bf16[1024,256]{1,0:T(8,128)(2,1)} %c_ref.5, bf16[8,128,256]{2,1,0:T(8,128)(2,1)} %bitcast.55, ...), custom_call_target="tpu_custom_call" | custom-call | flops 1073741824 | bytes 4194304 | tf_op jit(solution)/shard_map/pallas_call | solution.py:110
  148.9 4.5 %all-to-all-done.3 = f32[32,16,256]{2,1,0:T(8,128)S(1)} async-done(((f32[32,16,256]{2,1,0:T(8,128)}), f32[32,16,256]{2,1,0:T(8,128)S(1)}, u32[]{:S(2)}, u32[]{:S(2)}) %all-to-all-start.3) | async-done | bytes 524320 | tf_op jit(solution)/shard_map/all_to_all | solution.py:230
  153.4 0.7 slice_bitcast_fusion.g_ref
  154.8 2.9 %multiply_convert_fusion = f16[32,64,256]{2,1,0:T(8,128)(2,1)} fusion(f32[32,64,256]{2,1,0:T(8,128)} %shard_map.90, f32[256]{0:T(256)S(1)} %get-tuple-element.44), kind=kLoop, calls=%fused_computation.4 | loop fusion | flops 1048576 | bytes 3146752 | tf_op jit(solution)/shard_map/convert_element_type | solution.py:341
  157.6 5.3 %all-to-all-start.4 = ((f16[32,64,256]{2,1,0:T(8,128)(2,1)}), f16[32,64,256]{2,1,0:T(8,128)(2,1)S(1)}, u32[]{:S(2)}, u32[]{:S(2)}) async-start(f16[32,64,256]{2,1,0:T(8,128)(2,1)} %multiply_convert_fusion), calls=%async_computation.4 | async-start | bytes 2097152 | tf_op jit(solution)/shard_map/all_to_all | solution.py:230
  163.1 10.0 %shard_map.91.inverse_ref = f32[256,256]{1,0:T(8,128)} custom-call(f32[256,256]{1,0:T(8,128)} %slice_bitcast_fusion.g_ref, f32[256,256]{1,0:T(8,128)} %get-tuple-element.45.c_ref, f32[1,256]{1,0:T(1,128)} %bitcast.67), custom_call_target="tpu_custom_call" | custom-call | flops 10000000000 | bytes 1000000 | tf_op jit(solution)/shard_map/pallas_call | solution.py:211
  173.1 6.8 %all-to-all-done.4 = f16[32,64,256]{2,1,0:T(8,128)(2,1)S(1)} async-done(((f16[32,64,256]{2,1,0:T(8,128)(2,1)}), f16[32,64,256]{2,1,0:T(8,128)(2,1)S(1)}, u32[]{:S(2)}, u32[]{:S(2)}) %all-to-all-start.4) | async-done | bytes 1048608 | tf_op jit(solution)/shard_map/all_to_all | solution.py:230
  181.0 2.0 %shard_map.92 = f32[128,256]{1,0:T(8,128)} custom-call(f32[128,256]{1,0:T(8,128)} %pad_maximum_fusion.2.m_ref, f32[256,256]{1,0:T(8,128)} %shard_map.91.inverse_ref), custom_call_target="tpu_custom_call" | custom-call | tf_op jit(solution)/shard_map/pallas_call | solution.py:353
  (78 shorter events, 9.0 us)
Async XLA Ops:
  0.6 4.9 %collective-permute-start = (bf16[1,128,256]{2,1,0:T(8,128)(2,1)}, bf16[1,128,256]{2,1,0:T(8,128)(2,1)S(1)}, u32[]{:S(2)}, u32[]{:S(2)}) collective-permute-start(bf16[1,128,256]{2,1,0:T(8,128)(2,1)} %bitcast.58), channel_id=1, source_target_pairs={{0,64},{8,72},{16,80},{24,88},{32,96},{40,104},{48,112},{56,120},{... | collective-permute-start | bytes 196616 | tf_op jit(solution)/shard_map/ppermute | solution.py:33
  1.9 5.3 %collective-permute-start.1 = (bf16[1,128,256]{2,1,0:T(8,128)(2,1)}, bf16[1,128,256]{2,1,0:T(8,128)(2,1)S(1)}, u32[]{:S(2)}, u32[]{:S(2)}) collective-permute-start(bf16[1,128,256]{2,1,0:T(8,128)(2,1)} %bitcast.59), channel_id=1, source_target_pairs={{0,128},{8,136},{16,144},{24,152},{32,160},{40,168},{48,176},{56,1... | collective-permute-start | bytes 196616 | tf_op jit(solution)/shard_map/ppermute | solution.py:33
  4.4 3.9 %collective-permute-start.2 = (bf16[1,128,256]{2,1,0:T(8,128)(2,1)}, bf16[1,128,256]{2,1,0:T(8,128)(2,1)S(1)}, u32[]{:S(2)}, u32[]{:S(2)}) collective-permute-start(bf16[1,128,256]{2,1,0:T(8,128)(2,1)} %bitcast.60), channel_id=1, source_target_pairs={{0,192},{8,200},{16,208},{24,216},{32,224},{40,232},{48,240},{56,2... | collective-permute-start | bytes 196616 | tf_op jit(solution)/shard_map/ppermute | solution.py:33
  9.1 7.4 %collective-permute-start.3 = (bf16[4,128,256]{2,1,0:T(8,128)(2,1)S(1)}, bf16[4,128,256]{2,1,0:T(8,128)(2,1)S(1)}, u32[]{:S(2)}, u32[]{:S(2)}) collective-permute-start(bf16[4,128,256]{2,1,0:T(8,128)(2,1)S(1)} %pad_maximum_fusion), channel_id=1, source_target_pairs={{0,16},{8,24},{16,32},{24,40},{32,48},{40,56},{48,0},{56,8},{64,80... | collective-permute-start | bytes 786440 | tf_op jit(solution)/shard_map/ppermute | solution.py:33
  12.0 5.7 %collective-permute-start.5 = (bf16[4,128,256]{2,1,0:T(8,128)(2,1)S(1)}, bf16[4,128,256]{2,1,0:T(8,128)(2,1)S(1)}, u32[]{:S(2)}, u32[]{:S(2)}) collective-permute-start(bf16[4,128,256]{2,1,0:T(8,128)(2,1)S(1)} %pad_maximum_fusion), channel_id=1, source_target_pairs={{0,48},{8,56},{16,0},{24,8},{32,16},{40,24},{48,32},{56,40},{64,11... | collective-permute-start | bytes 786440 | tf_op jit(solution)/shard_map/ppermute | solution.py:33
  16.6 5.1 %collective-permute-start.4 = (bf16[2,128,256]{2,1,0:T(8,128)(2,1)S(1)}, bf16[2,128,256]{2,1,0:T(8,128)(2,1)S(1)}, u32[]{:S(2)}, u32[]{:S(2)}) collective-permute-start(bf16[2,128,256]{2,1,0:T(8,128)(2,1)S(1)} %slice.32), channel_id=1, source_target_pairs={{0,16},{8,24},{16,32},{24,40},{32,48},{40,56},{48,0},{56,8},{64,80... | collective-permute-start | bytes 393224 | tf_op jit(solution)/shard_map/ppermute | solution.py:33
  17.7 4.8 %collective-permute-start.6 = (bf16[2,128,256]{2,1,0:T(8,128)(2,1)S(1)}, bf16[2,128,256]{2,1,0:T(8,128)(2,1)S(1)}, u32[]{:S(2)}, u32[]{:S(2)}) collective-permute-start(bf16[2,128,256]{2,1,0:T(8,128)(2,1)S(1)} %slice.33), channel_id=1, source_target_pairs={{0,48},{8,56},{16,0},{24,8},{32,16},{40,24},{48,32},{56,40},{64,11... | collective-permute-start | bytes 393224 | tf_op jit(solution)/shard_map/ppermute | solution.py:33
  23.9 6.3 %collective-permute-start.7 = (bf16[16,128,256]{2,1,0:T(8,128)(2,1)}, bf16[16,128,256]{2,1,0:T(8,128)(2,1)S(1)}, u32[]{:S(2)}, u32[]{:S(2)}) collective-permute-start(bf16[16,128,256]{2,1,0:T(8,128)(2,1)} %get-tuple-element.27), channel_id=1, source_target_pairs={{0,8},{8,0},{16,24},{24,16},{32,40},{40,32},{48,56},{56,48},{64,72... | collective-permute-start | bytes 3145736 | tf_op jit(solution)/shard_map/ppermute | solution.py:33
  30.2 1.3 copy-start.2
  30.2 10.7 %copy-start.6 = (s32[1,1,16]{2,1,0:T(1,128)S(1)}, s32[1,1,16]{2,1,0:T(1,128)}, u32[]{:S(2)}) copy-start(s32[1,1,16]{2,1,0:T(1,128)} %param.9) | copy-start | bytes 196
  32.3 21.5 %all-to-all-start = ((f32[8,32,256]{2,1,0:T(8,128)}), f32[8,32,256]{2,1,0:T(8,128)S(1)}, u32[]{:S(2)}, u32[]{:S(2)}) async-start(f32[8,32,256]{2,1,0:T(8,128)} %broadcast_in_dim.54), calls=%async_computation | async-start | bytes 524288 | tf_op jit(solution)/shard_map/all_to_all | solution.py:230
  41.5 82.0 %copy-start.4 = (s32[16]{0:T(128)}, s32[16]{0:T(128)S(1)}, u32[]{:S(2)}) copy-start(s32[16]{0:T(128)S(1)} %get-tuple-element.21.owners_ref) | copy-start | bytes 196
  53.8 14.5 %copy-start.1 = (bf16[1024,256]{1,0:T(8,128)(2,1)S(1)}, bf16[1024,256]{1,0:T(8,128)(2,1)}, u32[]{:S(2)}) copy-start(bf16[1024,256]{1,0:T(8,128)(2,1)} %c_ref.5) | copy-start | bytes 1572868
  53.8 11.5 %collective-permute-start.8 = (f32[32,256]{1,0:T(8,128)S(1)}, f32[32,256]{1,0:T(8,128)S(1)}, u32[]{:S(2)}, u32[]{:S(2)}) collective-permute-start(f32[32,256]{1,0:T(8,128)S(1)} %reduce_sum.82), channel_id=1, source_target_pairs={{0,192},{8,200},{16,208},{24,216},{32,224},{40,232},{48,240},{56,2... | collective-permute-start | bytes 98312 | tf_op jit(solution)/shard_map/ppermute | solution.py:33
  53.9 11.4 %collective-permute-start.9 = (f32[32,256]{1,0:T(8,128)S(1)}, f32[32,256]{1,0:T(8,128)S(1)}, u32[]{:S(2)}, u32[]{:S(2)}) collective-permute-start(f32[32,256]{1,0:T(8,128)S(1)} %reduce_sum.82), channel_id=1, source_target_pairs={{0,128},{8,136},{16,144},{24,152},{32,160},{40,168},{48,176},{56,1... | collective-permute-start | bytes 98312 | tf_op jit(solution)/shard_map/ppermute | solution.py:33
  58.7 6.7 %collective-permute-start.10 = (f32[32,256]{1,0:T(8,128)S(1)}, f32[32,256]{1,0:T(8,128)S(1)}, u32[]{:S(2)}, u32[]{:S(2)}) collective-permute-start(f32[32,256]{1,0:T(8,128)S(1)} %reduce_sum.82), channel_id=1, source_target_pairs={{0,64},{8,72},{16,80},{24,88},{32,96},{40,104},{48,112},{56,120},{... | collective-permute-start | bytes 98312 | tf_op jit(solution)/shard_map/ppermute | solution.py:33
  58.7 31.6 %all-to-all-start.1 = ((f32[8,128,256]{2,1,0:T(8,128)}), f32[8,128,256]{2,1,0:T(8,128)S(1)}, u32[]{:S(2)}, u32[]{:S(2)}) async-start(f32[8,128,256]{2,1,0:T(8,128)} %bitcast.57), calls=%async_computation.1 | async-start | bytes 2097152 | tf_op jit(solution)/shard_map/all_to_all | solution.py:230
  65.5 2.8 %collective-permute-start.11 = (f32[128,256]{1,0:T(8,128)S(1)}, f32[128,256]{1,0:T(8,128)S(1)}, u32[]{:S(2)}, u32[]{:S(2)}) collective-permute-start(f32[128,256]{1,0:T(8,128)S(1)} %constant_dynamic-slice_fusion), channel_id=1, source_target_pairs={{0,8},{8,0},{16,24},{24,16},{32,40},{40,32},{48,56},{56,48},{64,72... | collective-permute-start | bytes 393224 | tf_op jit(solution)/shard_map/ppermute | solution.py:33
  91.0 32.0 %copy-start.5 = (s32[1,1,16]{2,1,0:T(1,128)S(1)}, s32[1,1,16]{2,1,0:T(1,128)}, u32[]{:S(2)}) copy-start(s32[1,1,16]{2,1,0:T(1,128)} %param.8) | copy-start | bytes 196
  92.9 7.6 %collective-permute-start.16 = (bf16[128,256]{1,0:T(8,128)(2,1)}, bf16[128,256]{1,0:T(8,128)(2,1)S(1)}, u32[]{:S(2)}, u32[]{:S(2)}) collective-permute-start(bf16[128,256]{1,0:T(8,128)(2,1)} %get-tuple-element.13), channel_id=1, source_target_pairs={{0,6},{1,7},{2,0},{3,1},{4,2},{5,3},{6,4},{7,5},{8,14},{9,15},{10,... | collective-permute-start | bytes 196616 | tf_op jit(solution)/shard_map/ppermute | solution.py:309
  92.9 9.2 %collective-permute-start.15 = (bf16[128,256]{1,0:T(8,128)(2,1)}, bf16[128,256]{1,0:T(8,128)(2,1)S(1)}, u32[]{:S(2)}, u32[]{:S(2)}) collective-permute-start(bf16[128,256]{1,0:T(8,128)(2,1)} %get-tuple-element.13), channel_id=1, source_target_pairs={{0,7},{1,0},{2,1},{3,2},{4,3},{5,4},{6,5},{7,6},{8,15},{9,8},{10,9... | collective-permute-start | bytes 196616 | tf_op jit(solution)/shard_map/ppermute | solution.py:309
  97.2 6.4 %collective-permute-start.13 = (bf16[128,256]{1,0:T(8,128)(2,1)}, bf16[128,256]{1,0:T(8,128)(2,1)S(1)}, u32[]{:S(2)}, u32[]{:S(2)}) collective-permute-start(bf16[128,256]{1,0:T(8,128)(2,1)} %get-tuple-element.13), channel_id=1, source_target_pairs={{0,2},{1,3},{2,4},{3,5},{4,6},{5,7},{6,0},{7,1},{8,10},{9,11},{10,... | collective-permute-start | bytes 196616 | tf_op jit(solution)/shard_map/ppermute | solution.py:309
  99.6 5.7 %collective-permute-start.12 = (bf16[128,256]{1,0:T(8,128)(2,1)}, bf16[128,256]{1,0:T(8,128)(2,1)S(1)}, u32[]{:S(2)}, u32[]{:S(2)}) collective-permute-start(bf16[128,256]{1,0:T(8,128)(2,1)} %get-tuple-element.13), channel_id=1, source_target_pairs={{0,1},{1,2},{2,3},{3,4},{4,5},{5,6},{6,7},{7,0},{8,9},{9,10},{10,1... | collective-permute-start | bytes 196616 | tf_op jit(solution)/shard_map/ppermute | solution.py:309
  102.1 11.5 %collective-permute-start.17 = (bf16[192,256]{1,0:T(8,128)(2,1)S(1)}, bf16[192,256]{1,0:T(8,128)(2,1)S(1)}, u32[]{:S(2)}, u32[]{:S(2)}) collective-permute-start(bf16[192,256]{1,0:T(8,128)(2,1)S(1)} %pad_maximum_fusion.4), channel_id=1, source_target_pairs={{0,6},{1,7},{2,0},{3,1},{4,2},{5,3},{6,4},{7,5},{8,14},{9,15},{10,... | collective-permute-start | bytes 294920 | tf_op jit(solution)/shard_map/ppermute | solution.py:309
  105.3 8.3 %collective-permute-start.14 = (bf16[192,256]{1,0:T(8,128)(2,1)S(1)}, bf16[192,256]{1,0:T(8,128)(2,1)S(1)}, u32[]{:S(2)}, u32[]{:S(2)}) collective-permute-start(bf16[192,256]{1,0:T(8,128)(2,1)S(1)} %pad_maximum_fusion.3), channel_id=1, source_target_pairs={{0,2},{1,3},{2,4},{3,5},{4,6},{5,7},{6,0},{7,1},{8,10},{9,11},{10,... | collective-permute-start | bytes 294920 | tf_op jit(solution)/shard_map/ppermute | solution.py:309
  113.7 10.0 %copy-start = (bf16[1024,256]{1,0:T(8,128)(2,1)}, bf16[1024,256]{1,0:T(8,128)(2,1)S(1)}, u32[]{:S(2)}) copy-start(bf16[1024,256]{1,0:T(8,128)(2,1)S(1)} %constant_dynamic-update-slice_fusion.25) | copy-start | bytes 1572868
  114.7 18.8 %all-to-all-start.2 = ((f32[32,8,256]{2,1,0:T(8,128)}), f32[32,8,256]{2,1,0:T(8,128)S(1)}, u32[]{:S(2)}, u32[]{:S(2)}) async-start(f32[32,8,256]{2,1,0:T(8,128)} %convolution_bitcast_fusion), calls=%async_computation.2 | async-start | bytes 524288 | tf_op jit(solution)/shard_map/all_to_all | solution.py:230
  134.4 19.0 %all-to-all-start.3 = ((f32[32,16,256]{2,1,0:T(8,128)}), f32[32,16,256]{2,1,0:T(8,128)S(1)}, u32[]{:S(2)}, u32[]{:S(2)}) async-start(f32[32,16,256]{2,1,0:T(8,128)} %broadcast_in_dim.89), calls=%async_computation.3 | async-start | bytes 1048576 | tf_op jit(solution)/shard_map/all_to_all | solution.py:230
  141.8 12.3 %copy-start.3 = (f32[256,256]{1,0:T(8,128)S(1)}, f32[256,256]{1,0:T(8,128)}, u32[]{:S(2)}) copy-start(f32[256,256]{1,0:T(8,128)} %get-tuple-element.45.c_ref) | copy-start | bytes 786436
  157.6 22.2 %all-to-all-start.4 = ((f16[32,64,256]{2,1,0:T(8,128)(2,1)}), f16[32,64,256]{2,1,0:T(8,128)(2,1)S(1)}, u32[]{:S(2)}, u32[]{:S(2)}) async-start(f16[32,64,256]{2,1,0:T(8,128)(2,1)} %multiply_convert_fusion), calls=%async_computation.4 | async-start | bytes 2097152 | tf_op jit(solution)/shard_map/all_to_all | solution.py:230

commit v2 on v1

--- a/solution.py
+++ b/solution.py
@@ -39,12 +39,6 @@
     )
 
 
-def begin(previous, out_ref):
-    @pl.when(pl.program_id(0) == 0)
-    def _():
-        out_ref[...] = previous[0][...] if previous else jnp.zeros_like(out_ref)
-
-
 def mixed_chunk(x_ref, u, k, bs, c_rows):
     part = x_ref[u, :, k * CHUNK * bs:(k + 1) * CHUNK * bs]
     mixed = lax.dot_general(
@@ -55,9 +49,13 @@
 
 def pass_one_kernel(first, rows_ref, picks_ref, depth_ref, count_ref, x_ref, c_ref, *rest):
     b_refs = rest[:UNROLL]
-    *previous, out_ref = rest[UNROLL:]
+    out_ref = rest[UNROLL]
     bs = x_ref.shape[1]
-    begin(previous, out_ref)
+
+    @pl.when(pl.program_id(0) == 0)
+    def _():
+        out_ref[...] = jnp.zeros_like(out_ref)
+
     for u in range(UNROLL):
         slot = first + pl.program_id(0) * UNROLL + u
 
@@ -74,11 +72,19 @@
 
 def pass_two_kernel(first, picks_ref, owners_ref, depth_ref, count_ref, x_ref, c_ref, *rest):
     a_refs = rest[:UNROLL]
-    *previous, out_ref = rest[UNROLL:]
+    _, out_ref, tile_ref, sem = rest[UNROLL:]
     bs = x_ref.shape[1]
-    begin(previous, out_ref)
+    step = pl.program_id(0)
+
+    def copy(u, slot):
+        return pltpu.make_async_copy(tile_ref.at[u], out_ref.at[owners_ref[slot]], sem.at[u])
+
     for u in range(UNROLL):
-        slot = first + pl.program_id(0) * UNROLL + u
+        slot = first + step * UNROLL + u
+
+        @pl.when((step > 0) & (slot - UNROLL < count_ref[0]))
+        def _():
+            copy(u, slot - UNROLL).wait()
 
         @pl.when(slot < count_ref[0])
         def _():
@@ -88,7 +94,15 @@
                 mixed = mixed_chunk(x_ref, u, k, bs, c_rows)
                 a_rows = a_refs[u][0, k * CHUNK:(k + 1) * CHUNK, :].astype(jnp.float32)
                 total = total + jnp.sum(mixed * a_rows[:, None, :], axis=0)
-            out_ref[owners_ref[slot]] = total
+            tile_ref[u] = total
+            copy(u, slot).start()
+
+    for u in range(UNROLL):
+        slot = first + step * UNROLL + u
+
+        @pl.when((step == pl.num_programs(0) - 1) & (slot < count_ref[0]))
+        def _():
+            copy(u, slot).wait()
 
 
 def run_pass(kernel, piece, pieces, tables, blocks, tiles, factor_c, out_tiles, use_first, previous=None):
@@ -97,6 +111,7 @@
     steps = slots // pieces // UNROLL
     start = piece * steps
     extra = [] if previous is None else [previous]
+    scratch = []
 
     def block_map(s, f, p, d, cnt):
         return (jnp.minimum(s + start, (cnt[0] - 1) // UNROLL), 0, 0)
@@ -107,6 +122,11 @@
         return (pick // TJ_DEV, pick % TJ_DEV, 0)
 
     whole = pl.BlockSpec((out_tiles, bs, rank), lambda s, f, p, d, cnt: (0, 0, 0))
+    aliases = {}
+    if extra:
+        whole = pl.BlockSpec(memory_space=pl.ANY)
+        scratch = [pltpu.VMEM((UNROLL, bs, rank), jnp.float32), pltpu.SemaphoreType.DMA((UNROLL,))]
+        aliases = {len(tables) + 2 + UNROLL: 0}
     return pl.pallas_call(
         functools.partial(kernel, start * UNROLL),
         out_shape=jax.ShapeDtypeStruct((out_tiles, bs, rank), jnp.float32),
@@ -122,7 +142,9 @@
             ]
             + [whole] * len(extra),
             out_specs=whole,
+            scratch_shapes=scratch,
         ),
+        input_output_aliases=aliases,
         compiler_params=pltpu.CompilerParams(dimension_semantics=("arbitrary",)),
         cost_estimate=pl.CostEstimate(
             flops=steps * UNROLL * wide_block * bs * rank * 2,
@@ -270,21 +292,24 @@
 
     gram_c = column_gram(factor_c)
 
-    packed = factor_b[None]
-    along_x = jnp.concatenate([packed] + [shift_wide(packed, k, 0, 0) for k in (1, 2, 3)], axis=0)
-    back = shift_wide(along_x, 0, 1, 0)
-    ahead = shift_wide(along_x, 0, 3, 0)
-    middle = [shift_wide(back[:NX // 2], 0, 1, 0), shift_wide(ahead[NX // 2:], 0, 3, 0)]
-    along_y = jnp.concatenate([along_x, back, *middle, ahead], axis=0)
-    gathered = jnp.concatenate([along_y, shift_wide(along_y, 0, 0, 1)], axis=0)
-
     def relative(owner):
         ox = owner // (NY * NC)
         oy = (owner // NC) % NY
         oc = owner % NC
         return ((c ^ oc) * NY + (y - oy) % NY) * NX + (x - ox) % NX
 
+    packed = factor_b[None]
+    along_x = jnp.concatenate([packed] + [shift_wide(packed, k, 0, 0) for k in (1, 2, 3)], axis=0)
+    back = shift_wide(along_x, 0, 1, 0)
+    ahead = shift_wide(along_x, 0, 3, 0)
+    a_pick = ((n - first_ids // TI_DEV) % n_narrow) * TI_DEV + first_ids % TI_DEV
     b_pick = relative(owners) * TJ_DEV + inside
+    empty = jnp.full((n_wide, bs, rank), jnp.minimum(count[0], 0), jnp.float32)
+    back, a_pick, b_pick, empty = lax.optimization_barrier((back, a_pick, b_pick, empty))
+    middle = [shift_wide(back[:NX // 2], 0, 1, 0), shift_wide(ahead[NX // 2:], 0, 3, 0)]
+    along_y = jnp.concatenate([along_x, back, *middle, ahead], axis=0)
+    gathered = jnp.concatenate([along_y, shift_wide(along_y, 0, 0, 1)], axis=0)
+
     tables = (first_ids, b_pick, depth_ids, count)
 
     gram_plane = column_gram(gathered.reshape(n_wide * rows, rank))
@@ -315,13 +340,12 @@
     a_all = jnp.concatenate(
         [a_half, back_1, back_2, back_34, ahead_34[rows:], ahead_34[:rows], ahead_2, ahead_1], axis=0
     ).reshape(n_narrow, rows, rank)
-    a_pick = ((n - first_ids // TI_DEV) % n_narrow) * TI_DEV + first_ids % TI_DEV
 
     tables = (a_pick, owners, depth_ids, count)
     gram_w = column_gram(a_all.reshape(n_narrow * rows, rank))
     arrived = exchange(gram_w.reshape(n_wide, share, rank), "wide")
     second_part = run_pass(
-        pass_two_kernel, 0, 2, tables, local_blocks, a_all, factor_c, n_wide, True
+        pass_two_kernel, 0, 2, tables, local_blocks, a_all, factor_c, n_wide, True, empty
     )
     second_part, arrived = lax.optimization_barrier((second_part, arrived))
     lanes = jnp.arange(rank, dtype=jnp.int32)

time: 184 us -> 181 us (0.984)
  the two profiles are of different devices: /device:TPU:33 before, /device:TPU:1 now
where the time goes in v2:
time: 181 us; the launch traced here: 180 us
  starting transfers between devices  65.6 us (36%)
  Pallas kernels  45.3 us (25%)
  waiting for transfers between devices  44.9 us (25%)
  local copies, waits for them, and re-layouts  12.4 us (7%)
  other arithmetic  7.74 us (4%)
  matrix products  2.85 us (2%)
    all_to_all x5, starting transfers between devices, exchange(): return lax.all_to_all(parts, axis, 0, 0, tiled=True)  35.7 us
    all_to_all x5, waiting for transfers between devices, exchange(): return lax.all_to_all(parts, axis, 0, 0, tiled=True)  31.6 us
    ppermute x12, starting transfers between devices, shift_wide(): return lax.ppermute(v, 'wide', pairs)  22.9 us
    pallas_call x3, Pallas kernels, run_pass(): pl.pallas_call(functools.partial(kernel, start * UNROLL), out_shape=jax.S...  21.4 us
    pallas_call x2, Pallas kernels, invert(): pl.pallas_call(invert_kernel, out_shape=jax.ShapeDtypeStruct((rank, rank)...  20 us
    unnamed x31, local copies, waits for them, and re-layouts  7.02 us
    ppermute x6, starting transfers between devices, shift_narrow(): lax.ppermute(v, 'narrow', [(i, (i + k) % n_narrow) for i in range(n_narro...  7.01 us
    ppermute x6, waiting for transfers between devices, shift_narrow(): lax.ppermute(v, 'narrow', [(i, (i + k) % n_narrow) for i in range(n_narro...  6.77 us
  transfers between devices with their start and end apart: 23, of which 12 were waited for; matrix products, arithmetic and copies ran while one was open for 6% of the time, Pallas kernels for 23%

profile of v2, /device:TPU:1, one launch (start us, length us, event | category | flops | bytes accessed | tf_op | source)
XLA Modules:
  0.0 180.5 jit_solution(8993540527173447056)
XLA Ops:
  0.6 2.1 %collective-permute-start = (bf16[1,128,256]{2,1,0:T(8,128)(2,1)}, bf16[1,128,256]{2,1,0:T(8,128)(2,1)S(1)}, u32[]{:S(2)}, u32[]{:S(2)}) collective-permute-start(bf16[1,128,256]{2,1,0:T(8,128)(2,1)} %bitcast.59), channel_id=1, source_target_pairs={{0,64},{8,72},{16,80},{24,88},{32,96},{40,104},{48,112},{56,120},{... | collective-permute-start | bytes 196616 | tf_op jit(solution)/shard_map/ppermute | solution.py:33
  2.7 2.5 %collective-permute-start.1 = (bf16[1,128,256]{2,1,0:T(8,128)(2,1)}, bf16[1,128,256]{2,1,0:T(8,128)(2,1)S(1)}, u32[]{:S(2)}, u32[]{:S(2)}) collective-permute-start(bf16[1,128,256]{2,1,0:T(8,128)(2,1)} %bitcast.60), channel_id=1, source_target_pairs={{0,128},{8,136},{16,144},{24,152},{32,160},{40,168},{48,176},{56,1... | collective-permute-start | bytes 196616 | tf_op jit(solution)/shard_map/ppermute | solution.py:33
  5.2 1.2 collective-permute-start.2
  6.3 1.5 constant_dynamic-update-slice_fusion.7
  8.0 0.8 collective-permute-done.2
  8.8 0.9 pad_maximum_fusion
  9.7 1.6 collective-permute-start.3
  11.3 1.2 multiply_add_fusion
  13.2 1.5 collective-permute-start.5
  16.0 1.1 collective-permute-done.3
  17.1 1.6 broadcast_in_dim.86.rest_2_
  19.6 2.5 %collective-permute-start.6 = (bf16[2,128,256]{2,1,0:T(8,128)(2,1)S(1)}, bf16[2,128,256]{2,1,0:T(8,128)(2,1)S(1)}, u32[]{:S(2)}, u32[]{:S(2)}) collective-permute-start(bf16[2,128,256]{2,1,0:T(8,128)(2,1)S(1)} %slice.32), channel_id=1, source_target_pairs={{0,48},{8,56},{16,0},{24,8},{32,16},{40,24},{48,32},{56,40},{64,11... | collective-permute-start | bytes 393224 | tf_op jit(solution)/shard_map/ppermute | solution.py:33
  22.9 0.9 collective-permute-done.4
  25.2 0.7 constant_dynamic-update-slice_fusion
  25.9 4.0 %collective-permute-start.7 = (bf16[16,128,256]{2,1,0:T(8,128)(2,1)}, bf16[16,128,256]{2,1,0:T(8,128)(2,1)S(1)}, u32[]{:S(2)}, u32[]{:S(2)}) collective-permute-start(bf16[16,128,256]{2,1,0:T(8,128)(2,1)} %get-tuple-element.35), channel_id=1, source_target_pairs={{0,8},{8,0},{16,24},{24,16},{32,40},{40,32},{48,56},{56,48},{64,72... | collective-permute-start | bytes 3145736 | tf_op jit(solution)/shard_map/ppermute | solution.py:33
  29.9 2.5 %collective-permute-done.7 = bf16[16,128,256]{2,1,0:T(8,128)(2,1)S(1)} collective-permute-done((bf16[16,128,256]{2,1,0:T(8,128)(2,1)}, bf16[16,128,256]{2,1,0:T(8,128)(2,1)S(1)}, u32[]{:S(2)}, u32[]{:S(2)}) %collective-permute-start.7) | collective-permute-done | bytes 1048608 | tf_op jit(solution)/shard_map/ppermute | solution.py:33
  32.6 0.7 convolution_bitcast_fusion.1
  34.6 8.2 %all-to-all-start = ((f32[8,32,256]{2,1,0:T(8,128)}), f32[8,32,256]{2,1,0:T(8,128)S(1)}, u32[]{:S(2)}, u32[]{:S(2)}) async-start(f32[8,32,256]{2,1,0:T(8,128)} %broadcast_in_dim.87), calls=%async_computation | async-start | bytes 524288 | tf_op jit(solution)/shard_map/all_to_all | solution.py:252
  42.8 10.0 %shard_map.86 = f32[16,64,256]{2,1,0:T(8,128)} custom-call(s32[16]{0:T(128)} %bitcast.68, s32[16]{0:T(128)} %get-tuple-element.14.picks_ref, s32[16]{0:T(128)} %bitcast.63, s32[1]{0:T(128)} %bitcast.48.count_ref, bf16[16,64,4096]{2,1,0:T(8,128)(2,1)} %bitcast.51, bf16[1024,256]{1,0:T(8,128)(2,1)} %c_ref.5, bf16[32,128,256]{2,1,0:T(8,128)(2,1)} %copy-done.2, ...), custom_call_target="tpu_custom_call" | custom-call | flops 2147483648 | bytes 8388608 | tf_op jit(solution)/shard_map/pallas_call | solution.py:130
  52.8 1.1 all-to-all-done
  53.9 2.2 %collective-permute-start.8 = (f32[32,256]{1,0:T(8,128)S(1)}, f32[32,256]{1,0:T(8,128)S(1)}, u32[]{:S(2)}, u32[]{:S(2)}) collective-permute-start(f32[32,256]{1,0:T(8,128)S(1)} %reduce_sum.82), channel_id=1, source_target_pairs={{0,192},{8,200},{16,208},{24,216},{32,224},{40,232},{48,240},{56,2... | collective-permute-start | bytes 98312 | tf_op jit(solution)/shard_map/ppermute | solution.py:33
  56.1 2.5 %collective-permute-start.9 = (f32[32,256]{1,0:T(8,128)S(1)}, f32[32,256]{1,0:T(8,128)S(1)}, u32[]{:S(2)}, u32[]{:S(2)}) collective-permute-start(f32[32,256]{1,0:T(8,128)S(1)} %reduce_sum.82), channel_id=1, source_target_pairs={{0,128},{8,136},{16,144},{24,152},{32,160},{40,168},{48,176},{56,1... | collective-permute-start | bytes 98312 | tf_op jit(solution)/shard_map/ppermute | solution.py:33
  59.3 7.1 %all-to-all-start.1 = ((f32[8,128,256]{2,1,0:T(8,128)}), f32[8,128,256]{2,1,0:T(8,128)S(1)}, u32[]{:S(2)}, u32[]{:S(2)}) async-start(f32[8,128,256]{2,1,0:T(8,128)} %bitcast.58), calls=%async_computation.1 | async-start | bytes 2097152 | tf_op jit(solution)/shard_map/all_to_all | solution.py:252
  66.5 1.8 collective-permute-start.11
  68.3 1.0 collective-permute-done.11
  69.3 1.0 pad_maximum_fusion.1
  70.9 10.0 %shard_map.87.inverse_ref = f32[256,256]{1,0:T(8,128)} custom-call(f32[256,256]{1,0:T(8,128)} %get-tuple-element.31.g_ref, f32[256,256]{1,0:T(8,128)} %get-tuple-element.53.c_ref, f32[1,256]{1,0:T(1,128)} %bitcast.66), custom_call_target="tpu_custom_call" | custom-call | flops 10000000000 | bytes 1000000 | tf_op jit(solution)/shard_map/pallas_call | solution.py:233
  80.9 14.6 %all-to-all-done.1 = f32[8,128,256]{2,1,0:T(8,128)S(1)} async-done(((f32[8,128,256]{2,1,0:T(8,128)}), f32[8,128,256]{2,1,0:T(8,128)S(1)}, u32[]{:S(2)}, u32[]{:S(2)}) %all-to-all-start.1) | async-done | bytes 1048608 | tf_op jit(solution)/shard_map/all_to_all | solution.py:252
  96.3 2.0 %shard_map.88 = (f32[128,256]{1,0:T(8,128)}, bf16[128,256]{1,0:T(8,128)(2,1)}) custom-call(f32[128,256]{1,0:T(8,128)} %reduce_sum.81.m_ref, f32[1,256]{1,0:T(1,128)} %bitcast.67, f32[256,256]{1,0:T(8,128)} %shard_map.87.inverse_ref), custom_call_target="tpu_custom_call" | custom-call | tf_op jit(solution)/shard_map/pallas_call | solution.py:329
  98.2 2.4 %collective-permute-start.13 = (bf16[128,256]{1,0:T(8,128)(2,1)}, bf16[128,256]{1,0:T(8,128)(2,1)S(1)}, u32[]{:S(2)}, u32[]{:S(2)}) collective-permute-start(bf16[128,256]{1,0:T(8,128)(2,1)} %get-tuple-element.20), channel_id=1, source_target_pairs={{0,2},{1,3},{2,4},{3,5},{4,6},{5,7},{6,0},{7,1},{8,10},{9,11},{10,... | collective-permute-start | bytes 196616 | tf_op jit(solution)/shard_map/ppermute | solution.py:334
  100.6 1.5 collective-permute-start.12
  102.1 0.9 constant_dynamic-update-slice_fusion.32
  103.0 1.3 collective-permute-start.17
  104.3 1.6 collective-permute-done.12
  105.9 1.9 %collective-permute-start.14 = (bf16[192,256]{1,0:T(8,128)(2,1)S(1)}, bf16[192,256]{1,0:T(8,128)(2,1)S(1)}, u32[]{:S(2)}, u32[]{:S(2)}) collective-permute-start(bf16[192,256]{1,0:T(8,128)(2,1)S(1)} %pad_maximum_fusion.3), channel_id=1, source_target_pairs={{0,2},{1,3},{2,4},{3,5},{4,6},{5,7},{6,0},{7,1},{8,10},{9,11},{10,... | collective-permute-start | bytes 294920 | tf_op jit(solution)/shard_map/ppermute | solution.py:334
  107.8 5.1 %collective-permute-done.14 = bf16[192,256]{1,0:T(8,128)(2,1)S(1)} collective-permute-done((bf16[192,256]{1,0:T(8,128)(2,1)S(1)}, bf16[192,256]{1,0:T(8,128)(2,1)S(1)}, u32[]{:S(2)}, u32[]{:S(2)}) %collective-permute-start.14) | collective-permute-done | bytes 98336 | tf_op jit(solution)/shard_map/ppermute | solution.py:334
  113.0 1.1 convolution_bitcast_fusion
  114.1 9.4 %all-to-all-start.2 = ((f32[32,8,256]{2,1,0:T(8,128)}), f32[32,8,256]{2,1,0:T(8,128)S(1)}, u32[]{:S(2)}, u32[]{:S(2)}) async-start(f32[32,8,256]{2,1,0:T(8,128)} %convolution_bitcast_fusion), calls=%async_computation.2 | async-start | bytes 524288 | tf_op jit(solution)/shard_map/all_to_all | solution.py:252
  123.6 9.1 %shard_map.89.rest_2_ = f32[32,64,256]{2,1,0:T(8,128)} custom-call(s32[16]{0:T(128)} %get-tuple-element.19.picks_ref, s32[16]{0:T(128)} %copy-done.4, s32[16]{0:T(128)} %bitcast.64, s32[1]{0:T(128)} %bitcast.49.count_ref, bf16[16,64,4096]{2,1,0:T(8,128)(2,1)} %bitcast.52, bf16[1024,256]{1,0:T(8,128)(2,1)} %c_ref.5, ...), custom_call_target="tpu_custom_call", output_to_operand_aliasing={{}: (8, {})} | custom-call | flops 1073741824 | bytes 4194304 | tf_op jit(solution)/shard_map/pallas_call | solution.py:130
  132.8 0.9 broadcast_in_dim.93
  133.6 7.4 %all-to-all-start.3 = ((f32[32,16,256]{2,1,0:T(8,128)}), f32[32,16,256]{2,1,0:T(8,128)S(1)}, u32[]{:S(2)}, u32[]{:S(2)}) async-start(f32[32,16,256]{2,1,0:T(8,128)} %broadcast_in_dim.93), calls=%async_computation.3 | async-start | bytes 1048576 | tf_op jit(solution)/shard_map/all_to_all | solution.py:252
  141.0 2.3 %shard_map.90 = f32[32,64,256]{2,1,0:T(8,128)} custom-call(s32[16]{0:T(128)} %get-tuple-element.19.picks_ref, s32[16]{0:T(128)} %copy-done.4, s32[16]{0:T(128)} %bitcast.65, s32[1]{0:T(128)} %bitcast.50.count_ref, bf16[16,64,4096]{2,1,0:T(8,128)(2,1)} %bitcast.53, bf16[1024,256]{1,0:T(8,128)(2,1)} %c_ref.5, ...), custom_call_target="tpu_custom_call", output_to_operand_aliasing={{}: (8, {})} | custom-call | flops 1073741824 | bytes 4194304 | tf_op jit(solution)/shard_map/pallas_call | solution.py:130
  143.3 9.3 %all-to-all-done.3 = f32[32,16,256]{2,1,0:T(8,128)S(1)} async-done(((f32[32,16,256]{2,1,0:T(8,128)}), f32[32,16,256]{2,1,0:T(8,128)S(1)}, u32[]{:S(2)}, u32[]{:S(2)}) %all-to-all-start.3) | async-done | bytes 524320 | tf_op jit(solution)/shard_map/all_to_all | solution.py:252
  154.0 2.9 %multiply_convert_fusion = f16[32,64,256]{2,1,0:T(8,128)(2,1)} fusion(f32[32,64,256]{2,1,0:T(8,128)} %shard_map.90, f32[256]{0:T(256)S(1)} %get-tuple-element.52), kind=kLoop, calls=%fused_computation.4 | loop fusion | flops 1048576 | bytes 3146752 | tf_op jit(solution)/shard_map/convert_element_type | solution.py:365
  156.8 3.7 %all-to-all-start.4 = ((f16[32,64,256]{2,1,0:T(8,128)(2,1)}), f16[32,64,256]{2,1,0:T(8,128)(2,1)S(1)}, u32[]{:S(2)}, u32[]{:S(2)}) async-start(f16[32,64,256]{2,1,0:T(8,128)(2,1)} %multiply_convert_fusion), calls=%async_computation.4 | async-start | bytes 2097152 | tf_op jit(solution)/shard_map/all_to_all | solution.py:252
  160.7 10.0 %shard_map.91.inverse_ref = f32[256,256]{1,0:T(8,128)} custom-call(f32[256,256]{1,0:T(8,128)} %slice_bitcast_fusion.g_ref, f32[256,256]{1,0:T(8,128)} %get-tuple-element.53.c_ref, f32[1,256]{1,0:T(1,128)} %bitcast.69), custom_call_target="tpu_custom_call" | custom-call | flops 10000000000 | bytes 1000000 | tf_op jit(solution)/shard_map/pallas_call | solution.py:233
  170.7 6.7 %all-to-all-done.4 = f16[32,64,256]{2,1,0:T(8,128)(2,1)S(1)} async-done(((f16[32,64,256]{2,1,0:T(8,128)(2,1)}), f16[32,64,256]{2,1,0:T(8,128)(2,1)S(1)}, u32[]{:S(2)}, u32[]{:S(2)}) %all-to-all-start.4) | async-done | bytes 1048608 | tf_op jit(solution)/shard_map/all_to_all | solution.py:252
  178.5 2.0 %shard_map.92 = f32[128,256]{1,0:T(8,128)} custom-call(f32[128,256]{1,0:T(8,128)} %pad_maximum_fusion.2.m_ref, f32[256,256]{1,0:T(8,128)} %shard_map.91.inverse_ref), custom_call_target="tpu_custom_call" | custom-call | tf_op jit(solution)/shard_map/pallas_call | solution.py:377
  (74 shorter events, 10.8 us)
Async XLA Ops:
  0.6 7.2 %collective-permute-start = (bf16[1,128,256]{2,1,0:T(8,128)(2,1)}, bf16[1,128,256]{2,1,0:T(8,128)(2,1)S(1)}, u32[]{:S(2)}, u32[]{:S(2)}) collective-permute-start(bf16[1,128,256]{2,1,0:T(8,128)(2,1)} %bitcast.59), channel_id=1, source_target_pairs={{0,64},{8,72},{16,80},{24,88},{32,96},{40,104},{48,112},{56,120},{... | collective-permute-start | bytes 196616 | tf_op jit(solution)/shard_map/ppermute | solution.py:33
  2.7 5.3 %collective-permute-start.1 = (bf16[1,128,256]{2,1,0:T(8,128)(2,1)}, bf16[1,128,256]{2,1,0:T(8,128)(2,1)S(1)}, u32[]{:S(2)}, u32[]{:S(2)}) collective-permute-start(bf16[1,128,256]{2,1,0:T(8,128)(2,1)} %bitcast.60), channel_id=1, source_target_pairs={{0,128},{8,136},{16,144},{24,152},{32,160},{40,168},{48,176},{56,1... | collective-permute-start | bytes 196616 | tf_op jit(solution)/shard_map/ppermute | solution.py:33
  5.2 3.6 %collective-permute-start.2 = (bf16[1,128,256]{2,1,0:T(8,128)(2,1)}, bf16[1,128,256]{2,1,0:T(8,128)(2,1)S(1)}, u32[]{:S(2)}, u32[]{:S(2)}) collective-permute-start(bf16[1,128,256]{2,1,0:T(8,128)(2,1)} %bitcast.61), channel_id=1, source_target_pairs={{0,192},{8,200},{16,208},{24,216},{32,224},{40,232},{48,240},{56,2... | collective-permute-start | bytes 196616 | tf_op jit(solution)/shard_map/ppermute | solution.py:33
  9.7 7.4 %collective-permute-start.3 = (bf16[4,128,256]{2,1,0:T(8,128)(2,1)S(1)}, bf16[4,128,256]{2,1,0:T(8,128)(2,1)S(1)}, u32[]{:S(2)}, u32[]{:S(2)}) collective-permute-start(bf16[4,128,256]{2,1,0:T(8,128)(2,1)S(1)} %pad_maximum_fusion), channel_id=1, source_target_pairs={{0,16},{8,24},{16,32},{24,40},{32,48},{40,56},{48,0},{56,8},{64,80... | collective-permute-start | bytes 786440 | tf_op jit(solution)/shard_map/ppermute | solution.py:33
  12.5 110.9 %copy-start.4 = (s32[16]{0:T(128)}, s32[16]{0:T(128)S(1)}, u32[]{:S(2)}) copy-start(s32[16]{0:T(128)S(1)} %get-tuple-element.29.owners_ref) | copy-start | bytes 196
  13.2 6.4 %collective-permute-start.5 = (bf16[4,128,256]{2,1,0:T(8,128)(2,1)S(1)}, bf16[4,128,256]{2,1,0:T(8,128)(2,1)S(1)}, u32[]{:S(2)}, u32[]{:S(2)}) collective-permute-start(bf16[4,128,256]{2,1,0:T(8,128)(2,1)S(1)} %pad_maximum_fusion), channel_id=1, source_target_pairs={{0,48},{8,56},{16,0},{24,8},{32,16},{40,24},{48,32},{56,40},{64,11... | collective-permute-start | bytes 786440 | tf_op jit(solution)/shard_map/ppermute | solution.py:33
  18.7 5.1 %collective-permute-start.4 = (bf16[2,128,256]{2,1,0:T(8,128)(2,1)S(1)}, bf16[2,128,256]{2,1,0:T(8,128)(2,1)S(1)}, u32[]{:S(2)}, u32[]{:S(2)}) collective-permute-start(bf16[2,128,256]{2,1,0:T(8,128)(2,1)S(1)} %slice.24), channel_id=1, source_target_pairs={{0,16},{8,24},{16,32},{24,40},{32,48},{40,56},{48,0},{56,8},{64,80... | collective-permute-start | bytes 393224 | tf_op jit(solution)/shard_map/ppermute | solution.py:33
  19.6 4.8 %collective-permute-start.6 = (bf16[2,128,256]{2,1,0:T(8,128)(2,1)S(1)}, bf16[2,128,256]{2,1,0:T(8,128)(2,1)S(1)}, u32[]{:S(2)}, u32[]{:S(2)}) collective-permute-start(bf16[2,128,256]{2,1,0:T(8,128)(2,1)S(1)} %slice.32), channel_id=1, source_target_pairs={{0,48},{8,56},{16,0},{24,8},{32,16},{40,24},{48,32},{56,40},{64,11... | collective-permute-start | bytes 393224 | tf_op jit(solution)/shard_map/ppermute | solution.py:33
  25.9 6.5 %collective-permute-start.7 = (bf16[16,128,256]{2,1,0:T(8,128)(2,1)}, bf16[16,128,256]{2,1,0:T(8,128)(2,1)S(1)}, u32[]{:S(2)}, u32[]{:S(2)}) collective-permute-start(bf16[16,128,256]{2,1,0:T(8,128)(2,1)} %get-tuple-element.35), channel_id=1, source_target_pairs={{0,8},{8,0},{16,24},{24,16},{32,40},{40,32},{48,56},{56,48},{64,72... | collective-permute-start | bytes 3145736 | tf_op jit(solution)/shard_map/ppermute | solution.py:33
  32.5 1.3 copy-start.2
  34.6 19.3 %all-to-all-start = ((f32[8,32,256]{2,1,0:T(8,128)}), f32[8,32,256]{2,1,0:T(8,128)S(1)}, u32[]{:S(2)}, u32[]{:S(2)}) async-start(f32[8,32,256]{2,1,0:T(8,128)} %broadcast_in_dim.87), calls=%async_computation | async-start | bytes 524288 | tf_op jit(solution)/shard_map/all_to_all | solution.py:252
  52.8 16.5 %copy-start.1 = (bf16[1024,256]{1,0:T(8,128)(2,1)S(1)}, bf16[1024,256]{1,0:T(8,128)(2,1)}, u32[]{:S(2)}) copy-start(bf16[1024,256]{1,0:T(8,128)(2,1)} %c_ref.5) | copy-start | bytes 1572868
  53.9 12.4 %collective-permute-start.8 = (f32[32,256]{1,0:T(8,128)S(1)}, f32[32,256]{1,0:T(8,128)S(1)}, u32[]{:S(2)}, u32[]{:S(2)}) collective-permute-start(f32[32,256]{1,0:T(8,128)S(1)} %reduce_sum.82), channel_id=1, source_target_pairs={{0,192},{8,200},{16,208},{24,216},{32,224},{40,232},{48,240},{56,2... | collective-permute-start | bytes 98312 | tf_op jit(solution)/shard_map/ppermute | solution.py:33
  56.1 10.3 %collective-permute-start.9 = (f32[32,256]{1,0:T(8,128)S(1)}, f32[32,256]{1,0:T(8,128)S(1)}, u32[]{:S(2)}, u32[]{:S(2)}) collective-permute-start(f32[32,256]{1,0:T(8,128)S(1)} %reduce_sum.82), channel_id=1, source_target_pairs={{0,128},{8,136},{16,144},{24,152},{32,160},{40,168},{48,176},{56,1... | collective-permute-start | bytes 98312 | tf_op jit(solution)/shard_map/ppermute | solution.py:33
  58.6 7.8 %collective-permute-start.10 = (f32[32,256]{1,0:T(8,128)S(1)}, f32[32,256]{1,0:T(8,128)S(1)}, u32[]{:S(2)}, u32[]{:S(2)}) collective-permute-start(f32[32,256]{1,0:T(8,128)S(1)} %reduce_sum.82), channel_id=1, source_target_pairs={{0,64},{8,72},{16,80},{24,88},{32,96},{40,104},{48,112},{56,120},{... | collective-permute-start | bytes 98312 | tf_op jit(solution)/shard_map/ppermute | solution.py:33
  59.3 36.2 %all-to-all-start.1 = ((f32[8,128,256]{2,1,0:T(8,128)}), f32[8,128,256]{2,1,0:T(8,128)S(1)}, u32[]{:S(2)}, u32[]{:S(2)}) async-start(f32[8,128,256]{2,1,0:T(8,128)} %bitcast.58), calls=%async_computation.1 | async-start | bytes 2097152 | tf_op jit(solution)/shard_map/all_to_all | solution.py:252
  66.5 2.8 %collective-permute-start.11 = (f32[128,256]{1,0:T(8,128)S(1)}, f32[128,256]{1,0:T(8,128)S(1)}, u32[]{:S(2)}, u32[]{:S(2)}) collective-permute-start(f32[128,256]{1,0:T(8,128)S(1)} %constant_dynamic-slice_fusion), channel_id=1, source_target_pairs={{0,8},{8,0},{16,24},{24,16},{32,40},{40,32},{48,56},{56,48},{64,72... | collective-permute-start | bytes 393224 | tf_op jit(solution)/shard_map/ppermute | solution.py:33
  98.2 4.7 %collective-permute-start.16 = (bf16[128,256]{1,0:T(8,128)(2,1)}, bf16[128,256]{1,0:T(8,128)(2,1)S(1)}, u32[]{:S(2)}, u32[]{:S(2)}) collective-permute-start(bf16[128,256]{1,0:T(8,128)(2,1)} %get-tuple-element.20), channel_id=1, source_target_pairs={{0,6},{1,7},{2,0},{3,1},{4,2},{5,3},{6,4},{7,5},{8,14},{9,15},{10,... | collective-permute-start | bytes 196616 | tf_op jit(solution)/shard_map/ppermute | solution.py:334
  98.2 4.7 %collective-permute-start.15 = (bf16[128,256]{1,0:T(8,128)(2,1)}, bf16[128,256]{1,0:T(8,128)(2,1)S(1)}, u32[]{:S(2)}, u32[]{:S(2)}) collective-permute-start(bf16[128,256]{1,0:T(8,128)(2,1)} %get-tuple-element.20), channel_id=1, source_target_pairs={{0,7},{1,0},{2,1},{3,2},{4,3},{5,4},{6,5},{7,6},{8,15},{9,8},{10,9... | collective-permute-start | bytes 196616 | tf_op jit(solution)/shard_map/ppermute | solution.py:334
  98.2 6.0 %collective-permute-start.13 = (bf16[128,256]{1,0:T(8,128)(2,1)}, bf16[128,256]{1,0:T(8,128)(2,1)S(1)}, u32[]{:S(2)}, u32[]{:S(2)}) collective-permute-start(bf16[128,256]{1,0:T(8,128)(2,1)} %get-tuple-element.20), channel_id=1, source_target_pairs={{0,2},{1,3},{2,4},{3,5},{4,6},{5,7},{6,0},{7,1},{8,10},{9,11},{10,... | collective-permute-start | bytes 196616 | tf_op jit(solution)/shard_map/ppermute | solution.py:334
  100.6 5.3 %collective-permute-start.12 = (bf16[128,256]{1,0:T(8,128)(2,1)}, bf16[128,256]{1,0:T(8,128)(2,1)S(1)}, u32[]{:S(2)}, u32[]{:S(2)}) collective-permute-start(bf16[128,256]{1,0:T(8,128)(2,1)} %get-tuple-element.20), channel_id=1, source_target_pairs={{0,1},{1,2},{2,3},{3,4},{4,5},{5,6},{6,7},{7,0},{8,9},{9,10},{10,1... | collective-permute-start | bytes 196616 | tf_op jit(solution)/shard_map/ppermute | solution.py:334
  103.0 10.0 %collective-permute-start.17 = (bf16[192,256]{1,0:T(8,128)(2,1)S(1)}, bf16[192,256]{1,0:T(8,128)(2,1)S(1)}, u32[]{:S(2)}, u32[]{:S(2)}) collective-permute-start(bf16[192,256]{1,0:T(8,128)(2,1)S(1)} %pad_maximum_fusion.4), channel_id=1, source_target_pairs={{0,6},{1,7},{2,0},{3,1},{4,2},{5,3},{6,4},{7,5},{8,14},{9,15},{10,... | collective-permute-start | bytes 294920 | tf_op jit(solution)/shard_map/ppermute | solution.py:334
  105.9 7.0 %collective-permute-start.14 = (bf16[192,256]{1,0:T(8,128)(2,1)S(1)}, bf16[192,256]{1,0:T(8,128)(2,1)S(1)}, u32[]{:S(2)}, u32[]{:S(2)}) collective-permute-start(bf16[192,256]{1,0:T(8,128)(2,1)S(1)} %pad_maximum_fusion.3), channel_id=1, source_target_pairs={{0,2},{1,3},{2,4},{3,5},{4,6},{5,7},{6,0},{7,1},{8,10},{9,11},{10,... | collective-permute-start | bytes 294920 | tf_op jit(solution)/shard_map/ppermute | solution.py:334
  113.0 10.5 %copy-start = (bf16[1024,256]{1,0:T(8,128)(2,1)}, bf16[1024,256]{1,0:T(8,128)(2,1)S(1)}, u32[]{:S(2)}) copy-start(bf16[1024,256]{1,0:T(8,128)(2,1)S(1)} %constant_dynamic-update-slice_fusion.25) | copy-start | bytes 1572868
  114.1 18.6 %all-to-all-start.2 = ((f32[32,8,256]{2,1,0:T(8,128)}), f32[32,8,256]{2,1,0:T(8,128)S(1)}, u32[]{:S(2)}, u32[]{:S(2)}) async-start(f32[32,8,256]{2,1,0:T(8,128)} %convolution_bitcast_fusion), calls=%async_computation.2 | async-start | bytes 524288 | tf_op jit(solution)/shard_map/all_to_all | solution.py:252
  133.6 19.0 %all-to-all-start.3 = ((f32[32,16,256]{2,1,0:T(8,128)}), f32[32,16,256]{2,1,0:T(8,128)S(1)}, u32[]{:S(2)}, u32[]{:S(2)}) async-start(f32[32,16,256]{2,1,0:T(8,128)} %broadcast_in_dim.93), calls=%async_computation.3 | async-start | bytes 1048576 | tf_op jit(solution)/shard_map/all_to_all | solution.py:252
  141.0 12.3 %copy-start.3 = (f32[256,256]{1,0:T(8,128)S(1)}, f32[256,256]{1,0:T(8,128)}, u32[]{:S(2)}) copy-start(f32[256,256]{1,0:T(8,128)} %get-tuple-element.53.c_ref) | copy-start | bytes 786436
  156.8 20.5 %all-to-all-start.4 = ((f16[32,64,256]{2,1,0:T(8,128)(2,1)}), f16[32,64,256]{2,1,0:T(8,128)(2,1)S(1)}, u32[]{:S(2)}, u32[]{:S(2)}) async-start(f16[32,64,256]{2,1,0:T(8,128)(2,1)} %multiply_convert_fusion), calls=%async_computation.4 | async-start | bytes 2097152 | tf_op jit(solution)/shard_map/all_to_all | solution.py:252
